TPU v7x, 256 devices: a whole 4x4x8 slice. The times are simulated.
256 devices in a mesh: ctx: 128 (over z, y, x), head: 2 (over core).
Axes of the slice: x: 4, y: 4, z: 8, core: 2. Of those that a mesh axis runs over, the one named last changes fastest.
Arguments:
- queries: bfloat16 [32768, 4096], P('ctx', 'head'), may hold values from -6.5 to 6.5
- keyval: bfloat16 [2, 32768, 1024], P(None, 'ctx', 'head'), may hold values from -6 to 6
- out_gain: float32 [4096], P('head'), may hold values from 0.1 to 1.9
Outputs:
- attended: bfloat16 [32768, 4096], P('ctx', 'head')
All inputs are finite; a program needn't handle non-finite values.
Results may differ from a plain program's by a relative error of at most 0.0049.
Values may be sent and summed in bfloat16 or wider, within the bound.
No kernel may reach another device: no remote copies, remote signals or barrier semaphores. Data moves between devices by JAX's collectives and lax.ppermute only.
A program may use at most 64 MiB of HBM per device.

v0:
```python
import functools

import jax
import jax.numpy as jnp
from jax import lax
from jax.experimental import pallas as pl
from jax.experimental.pallas import tpu as pltpu
from jax.sharding import PartitionSpec as P

HEADS = 32
HD = 128
BLK = 128
NZ, NY, NX = 8, 4, 4
NEG = -1e30
FACTOR = HD ** (-0.5) * 1.4426950408889634
VMEM = pl.BlockSpec(memory_space=pltpu.VMEM)
PARAMS = pltpu.CompilerParams(vmem_limit_bytes=16 << 20)


def on_chip(value):
    return pltpu.with_memory_space_constraint(value, pltpu.VMEM)


def ring(dz, dy, dx):
    return [
        (
            (z * NY + y) * NX + x,
            ((z + dz) % NZ * NY + (y + dy) % NY) * NX + (x + dx) % NX,
        )
        for z in range(NZ)
        for y in range(NY)
        for x in range(NX)
    ]


def send(value, dz, dy, dx):
    return lax.ppermute(value, "ctx", ring(dz, dy, dx))


def lanes(index):
    return pl.ds(index * HD if isinstance(index, int) else pl.multiple_of(index * HD, HD), HD)


def triangle():
    row = lax.broadcasted_iota(jnp.int32, (BLK, BLK), 0)
    col = lax.broadcasted_iota(jnp.int32, (BLK, BLK), 1)
    return jnp.where(row >= col, 0.0, NEG).astype(jnp.float32)


def gather_slots(panels, slots, g):
    ones = jnp.ones((BLK, HD), jnp.bfloat16)
    cut = lambda ref, j: ref[j * BLK : (j + 1) * BLK, lanes(g)]
    keys = jnp.concatenate([cut(panels[i][0], j) for i, j in slots], axis=0)
    vals = [jnp.concatenate([cut(panels[i][1], j), ones], axis=1) for i, j in slots]
    return keys, jnp.concatenate(vals, axis=0)


def score_parts(query, keys, masks):
    raw = lax.dot_general(query, keys, (((1,), (1,)), ((), ())), preferred_element_type=jnp.float32)
    parts = [raw[:, n * BLK : (n + 1) * BLK] for n in range(len(masks))]
    parts = [part if mask is None else part + mask for part, mask in zip(parts, masks)]
    top = jnp.max(functools.reduce(jnp.maximum, parts), axis=1, keepdims=True)
    return parts, top


def weigh(parts, top, vals):
    probs = [jnp.exp2((part - top) * FACTOR).astype(jnp.bfloat16) for part in parts]
    probs = jnp.concatenate(probs, axis=1)
    return lax.dot_general(probs, vals, (((1,), (0,)), ((), ())), preferred_element_type=jnp.float32)


def masks_of(slots, b):
    tri = triangle()
    place = lax.axis_index("ctx")
    masks = []
    for i, j in slots:
        if i == 0:
            masks.append(None if j == b else tri)
        else:
            masks.append(tri + jnp.where(place >= 2 ** (i - 1), 0.0, NEG))
    return masks


def split_kernel(kv_ref, k_ref, v_ref, sems):
    copies = [pltpu.make_async_copy(kv_ref.at[n], ref, sems.at[n]) for n, ref in enumerate((k_ref, v_ref))]
    for copy in copies:
        copy.start()
    for copy in copies:
        copy.wait()


def choose(moved, come_ref, own_ref, out_ref):
    @pl.when(moved)
    def _():
        out_ref[...] = come_ref[...]

    @pl.when(jnp.logical_not(moved))
    def _():
        out_ref[...] = own_ref[...]


def reaches(test):
    shift, least = test
    return ((lax.axis_index("ctx") >> shift) & 3) >= least


def pick_kernel(come_ref, own_ref, *outs, tests):
    for out_ref, test in zip(outs, tests):
        choose(reaches(test), come_ref, own_ref, out_ref)


def pick_both_kernel(come_k_ref, own_k_ref, come_v_ref, own_v_ref, near_ref, far_ref):
    choose(reaches(ROWS), come_v_ref, own_v_ref, near_ref)
    far = reaches(HALF_ROWS)
    choose(far, come_k_ref, own_k_ref, far_ref.at[0])
    choose(far, come_v_ref, own_v_ref, far_ref.at[1])


def stage_kernel(source_ref, *refs, ids, group, first, last):
    panels = {}
    q_ref = refs[-2] if first else source_ref
    for i in ids:
        if i == WHOLE:
            panels[i], refs = (refs[0].at[0], refs[0].at[1]), refs[1:]
        else:
            panels[i], refs = refs[:2], refs[2:]
    if not first:
        old_acc_ref, old_top_ref = refs[:2]
        refs = refs[2:]
    if last:
        comb_ref, sq_ref, total_ref = refs
        total_ref[...] = jnp.zeros_like(total_ref)
    else:
        acc_ref, top_ref = refs[:2]
    if first:
        width = group * HD
        loads = [
            pltpu.make_async_copy(source_ref.at[:, part], q_ref.at[:, part], refs[-1].at[n])
            for n, part in enumerate(pl.ds(n * width, width) for n in range(q_ref.shape[1] // width))
        ]
        for load in loads:
            load.start()

    def body(g, carry):
        for b in range(2):
            rows = slice(b * BLK, (b + 1) * BLK)
            slots = [(i, b) for i in ids]
            if b and 0 in ids:
                slots = slots + [(0, 0)]
            if not b and 1 in ids:
                slots = slots + [(1, 1)]
            masks = masks_of(slots, b)
            keys, vals = gather_slots(panels, slots, g)
            if last:
                total = total_ref[rows, :]
            for h in range(group):
                head = g * group + h
                unit = head * 2 + b
                parts, top = score_parts(q_ref[rows, lanes(head)], keys, masks)
                if first:
                    acc = weigh(parts, top, vals)
                else:
                    old = old_top_ref[unit]
                    top = jnp.maximum(old, top)
                    scale = jnp.exp2((old - top) * FACTOR)
                    both = weigh(parts, top, vals)
                    acc = old_acc_ref[unit] * jnp.concatenate([scale, scale], axis=1) + both
                if last:
                    comb = acc[:, :HD] / acc[:, HD:]
                    comb_ref[rows, lanes(head)] = comb
                    total = total + comb * comb
                else:
                    acc_ref[unit] = acc
                    top_ref[unit] = jnp.broadcast_to(top, (BLK, HD))
            if last:
                total_ref[rows, :] = total
        return carry

    if first:
        for g, load in enumerate(loads):
            load.wait()
            body(g, 0)
    else:
        lax.fori_loop(0, q_ref.shape[1] // HD // group, body, 0, unroll=UNROLL)
    if last:
        sq_ref[...] = lax.dot_general(
            jnp.ones((8, HD), jnp.float32),
            total_ref[...],
            (((1,), (1,)), ((), ())),
            preferred_element_type=jnp.float32,
            precision=lax.Precision.HIGHEST,
        )


def norm_kernel(comb_ref, mine_ref, other_ref, gain_ref, out_ref, buf, sems):
    rows, width = comb_ref.shape
    square_sum = mine_ref[...] + other_ref[...]
    inverse = lax.rsqrt(square_sum / (HEADS * HD) + 1e-06)[:1]
    inverse = jnp.transpose(jnp.broadcast_to(inverse, (HD, rows)))
    inverse = jnp.concatenate([inverse] * (width // HD), axis=1)
    step = rows // 4
    copies = []
    for n in range(4):
        part = slice(n * step, (n + 1) * step)
        buf[part, :] = (comb_ref[part, :] * inverse[part] * gain_ref[...]).astype(jnp.bfloat16)
        copies.append(pltpu.make_async_copy(buf.at[part], out_ref.at[part], sems.at[n]))
        copies[-1].start()
    for copy in copies:
        copy.wait()


def split(keyval):
    half = pltpu.VMEM(keyval.shape[1:], keyval.dtype)
    pair = pl.pallas_call(
        split_kernel,
        in_specs=[pl.BlockSpec(memory_space=pltpu.HBM)],
        out_specs=[VMEM, VMEM],
        out_shape=[half, half],
        scratch_shapes=[pltpu.SemaphoreType.DMA((2,))],
        compiler_params=PARAMS,
        name="split",
    )(pltpu.with_memory_space_constraint(keyval, pltpu.HBM))
    return [on_chip(half) for half in pair]


def pick(come, own, *tests):
    outs = pl.pallas_call(
        functools.partial(pick_kernel, tests=tests),
        in_specs=[VMEM, VMEM],
        out_specs=[VMEM] * len(tests),
        out_shape=[pltpu.VMEM(own.shape, own.dtype)] * len(tests),
        compiler_params=PARAMS,
        name="pick",
    )(on_chip(come), own)
    return [on_chip(out) for out in outs]


def pick_both(come_k, own_k, come_v, own_v):
    outs = pl.pallas_call(
        pick_both_kernel,
        in_specs=[VMEM] * 4,
        out_specs=[VMEM] * 2,
        out_shape=[pltpu.VMEM(own_v.shape, own_v.dtype), pltpu.VMEM((2, *own_v.shape), own_v.dtype)],
        compiler_params=PARAMS,
        name="pick_both",
    )(on_chip(come_k), own_k, on_chip(come_v), own_v)
    return [on_chip(out) for out in outs]


def attend(queries, panels, ids, group, state, last):
    rows, width = queries.shape
    count = width // HD * (rows // BLK)
    if last:
        shapes = [pltpu.VMEM((rows, width), jnp.float32), pltpu.VMEM((8, rows), jnp.float32)]
    else:
        shapes = [pltpu.VMEM((count, BLK, 2 * HD), jnp.float32), pltpu.VMEM((count, BLK, HD), jnp.float32)]
    scratch = [pltpu.VMEM((rows, HD), jnp.float32)] if last else []
    first = not state
    halves = [half for i in ids for half in panels[i]]
    source = VMEM
    if first:
        shapes.append(pltpu.VMEM((rows, width), jnp.bfloat16))
        scratch.append(pltpu.SemaphoreType.DMA((width // HD // group,)))
        source = pl.BlockSpec(memory_space=pltpu.HBM)
    outs = pl.pallas_call(
        functools.partial(stage_kernel, ids=ids, group=group, first=first, last=last),
        in_specs=[source] + [VMEM] * (len(halves) + len(state)),
        out_specs=[VMEM] * len(shapes),
        out_shape=shapes,
        scratch_shapes=scratch,
        compiler_params=PARAMS,
        name="stage",
    )(queries, *halves, *state)
    return [on_chip(out) for out in outs]


UNROLL = 2
WHOLE = 4
STAGES = ((0,), (5, 3), (6, 1), (4, 2, 7))
ROWS, HALF_ROWS, COLS, HALF_COLS = (2, 3), (2, 2), (0, 3), (0, 2)


def local(queries, keyval, out_gain):
    tok_rows, width = queries.shape
    group = width // keyval.shape[2]
    own = split(keyval)
    r16 = [send(own[0], 1, 0, 0), send(own[1], 1, 0, 0)]
    mid = send(own[1], -1, 0, 0)
    r32 = [send(r16[0], 1, 0, 0), send(r16[1], 1, 0, 0)]
    r64 = [send(r32[0], 2, 0, 0), send(mid, -3, 0, 0)]
    (near,) = pick(r16[0], own[0], ROWS)
    r4k = send(near, 0, 1, 0)
    near, far = pick_both(r16[0], own[0], r16[1], own[1])
    r4 = [r4k, send(near, 0, 1, 0)]
    r8 = [send(far, 0, 2, 0)]
    near, far = pick(r4[0], own[0], COLS, HALF_COLS)
    r1k = send(near, 0, 0, 1)
    r2k = send(send(far, 0, 0, -1), 0, 0, -1)
    near, far = pick(r4[1], own[1], COLS, HALF_COLS)
    r1 = [r1k, send(near, 0, 0, 1)]
    r2 = [r2k, send(far, 0, 0, 2)]
    panels = [[on_chip(half) for half in panel] for panel in (own, r1, r2, r4, r8, r16, r32, r64)]
    query = pltpu.with_memory_space_constraint(queries, pltpu.HBM)
    state = []
    for n, ids in enumerate(STAGES):
        state = attend(query, panels, ids, group, state, n == len(STAGES) - 1)
        if n == 0:
            *state, query = state
    comb, squares = state
    other = on_chip(lax.ppermute(squares, "head", [(0, 1), (1, 0)]))
    return pl.pallas_call(
        norm_kernel,
        in_specs=[VMEM] * 4,
        out_specs=pl.BlockSpec(memory_space=pl.ANY),
        out_shape=jax.ShapeDtypeStruct((tok_rows, width), jnp.bfloat16),
        scratch_shapes=[pltpu.VMEM((tok_rows, width), jnp.bfloat16), pltpu.SemaphoreType.DMA((4,))],
        compiler_params=PARAMS,
        name="norm",
    )(comb, squares, other, on_chip(out_gain[None, :]))


def solution(mesh):
    in_specs = (P("ctx", "head"), P(None, "ctx", "head"), P("head"))
    out_specs = P("ctx", "head")
    return jax.shard_map(local, mesh=mesh, in_specs=in_specs, out_specs=out_specs, check_vma=False)
```

profile of v0, /device:TPU:81, one launch (start us, length us, event | category | flops | bytes accessed | tf_op | source)
XLA Modules:
  0.0 73.5 jit_solution(1259186441948189493)
XLA Ops:
  0.0 1.0 %split.1 = (bf16[256,512]{1,0:T(8,128)(2,1)S(1)}, bf16[256,512]{1,0:T(8,128)(2,1)S(1)}) custom-call(bf16[2,256,512]{2,1,0:T(8,128)(2,1)} %kv_ref.1), custom_call_target="tpu_custom_call" | custom-call | tf_op jit(solution)/shard_map/split/pallas_call | solution.py:214
  1.1 1.7 %collective-permute-start = (bf16[256,512]{1,0:T(8,128)(2,1)S(1)}, bf16[256,512]{1,0:T(8,128)(2,1)S(1)}, u32[]{:S(2)}, u32[]{:S(2)}) collective-permute-start(bf16[256,512]{1,0:T(8,128)(2,1)S(1)} %get-tuple-element.22.refs_0_.own_k_ref.own_ref), channel_id=1, source_target_pairs={{0,32},{2,34},{4,36},{6,38},{8,40},{10,42},{12,44},{14,46},{16,48}... | collective-permute-start | bytes 786440 | tf_op jit(solution)/shard_map/ppermute | solution.py:37
  2.8 2.8 %collective-permute-start.1 = (bf16[256,512]{1,0:T(8,128)(2,1)S(1)}, bf16[256,512]{1,0:T(8,128)(2,1)S(1)}, u32[]{:S(2)}, u32[]{:S(2)}) collective-permute-start(bf16[256,512]{1,0:T(8,128)(2,1)S(1)} %get-tuple-element.23.refs_1_.own_v_ref.own_ref), channel_id=1, source_target_pairs={{0,32},{2,34},{4,36},{6,38},{8,40},{10,42},{12,44},{14,46},{16,48}... | collective-permute-start | bytes 786440 | tf_op jit(solution)/shard_map/ppermute | solution.py:37
  5.6 2.7 %collective-permute-done.come_k_ref.come_ref.refs_0_ = bf16[256,512]{1,0:T(8,128)(2,1)S(1)} collective-permute-done((bf16[256,512]{1,0:T(8,128)(2,1)S(1)}, bf16[256,512]{1,0:T(8,128)(2,1)S(1)}, u32[]{:S(2)}, u32[]{:S(2)}) %collective-permute-start) | collective-permute-done | bytes 262176 | tf_op jit(solution)/shard_map/ppermute | solution.py:37
  8.3 5.6 %collective-permute-done.1.come_v_ref.refs_1_ = bf16[256,512]{1,0:T(8,128)(2,1)S(1)} collective-permute-done((bf16[256,512]{1,0:T(8,128)(2,1)S(1)}, bf16[256,512]{1,0:T(8,128)(2,1)S(1)}, u32[]{:S(2)}, u32[]{:S(2)}) %collective-permute-start.1) | collective-permute-done | bytes 262176 | tf_op jit(solution)/shard_map/ppermute | solution.py:37
  13.9 0.1 pick_both.1
  14.0 1.1 %collective-permute-start.6 = (bf16[256,512]{1,0:T(8,128)(2,1)S(1)}, bf16[256,512]{1,0:T(8,128)(2,1)S(1)}, u32[]{:S(2)}, u32[]{:S(2)}) collective-permute-start(bf16[256,512]{1,0:T(8,128)(2,1)S(1)} %get-tuple-element.27), channel_id=1, source_target_pairs={{0,8},{2,10},{4,12},{6,14},{8,16},{10,18},{12,20},{14,22},{16,24},... | collective-permute-start | bytes 786440 | tf_op jit(solution)/shard_map/ppermute | solution.py:37
  15.1 0.1 collective-permute-start.3
  15.2 0.1 collective-permute-start.10
  15.3 2.4 %collective-permute-start.8 = (bf16[256,512]{1,0:T(8,128)(2,1)S(1)}, bf16[256,512]{1,0:T(8,128)(2,1)S(1)}, u32[]{:S(2)}, u32[]{:S(2)}) collective-permute-start(bf16[256,512]{1,0:T(8,128)(2,1)S(1)} %collective-permute-done.come_k_ref.come_ref.refs_0_), channel_id=1, source_target_pairs={{0,32},{2,34},{4,36},{6,38},{8,40},{10,42},{12,44},{14,46},{16,48}... | collective-permute-start | bytes 786440 | tf_op jit(solution)/shard_map/ppermute | solution.py:37
  17.6 1.5 %collective-permute-start.2 = (bf16[2,256,512]{2,1,0:T(8,128)(2,1)S(1)}, bf16[2,256,512]{2,1,0:T(8,128)(2,1)S(1)}, u32[]{:S(2)}, u32[]{:S(2)}) collective-permute-start(bf16[2,256,512]{2,1,0:T(8,128)(2,1)S(1)} %get-tuple-element.25), channel_id=1, source_target_pairs={{0,16},{2,18},{4,20},{6,22},{8,24},{10,26},{12,28},{14,30},{16,0},... | collective-permute-start | bytes 1572872 | tf_op jit(solution)/shard_map/ppermute | solution.py:37
  19.1 1.3 %collective-permute-done.6.come_ref.refs_3_ = bf16[256,512]{1,0:T(8,128)(2,1)S(1)} collective-permute-done((bf16[256,512]{1,0:T(8,128)(2,1)S(1)}, bf16[256,512]{1,0:T(8,128)(2,1)S(1)}, u32[]{:S(2)}, u32[]{:S(2)}) %collective-permute-start.6) | collective-permute-done | bytes 262176 | tf_op jit(solution)/shard_map/ppermute | solution.py:37
  20.4 2.3 %collective-permute-start.12 = (bf16[256,512]{1,0:T(8,128)(2,1)S(1)}, bf16[256,512]{1,0:T(8,128)(2,1)S(1)}, u32[]{:S(2)}, u32[]{:S(2)}) collective-permute-start(bf16[256,512]{1,0:T(8,128)(2,1)S(1)} %collective-permute-done.1.come_v_ref.refs_1_), channel_id=1, source_target_pairs={{0,32},{2,34},{4,36},{6,38},{8,40},{10,42},{12,44},{14,46},{16,48}... | collective-permute-start | bytes 786440 | tf_op jit(solution)/shard_map/ppermute | solution.py:37
  22.7 3.4 %collective-permute-done.3.come_ref.refs_2_ = bf16[256,512]{1,0:T(8,128)(2,1)S(1)} collective-permute-done((bf16[256,512]{1,0:T(8,128)(2,1)S(1)}, bf16[256,512]{1,0:T(8,128)(2,1)S(1)}, u32[]{:S(2)}, u32[]{:S(2)}) %collective-permute-start.3) | collective-permute-done | bytes 262176 | tf_op jit(solution)/shard_map/ppermute | solution.py:37
  26.1 1.2 %collective-permute-start.14 = (bf16[256,512]{1,0:T(8,128)(2,1)S(1)}, bf16[256,512]{1,0:T(8,128)(2,1)S(1)}, u32[]{:S(2)}, u32[]{:S(2)}) collective-permute-start(bf16[256,512]{1,0:T(8,128)(2,1)S(1)} %get-tuple-element.30), channel_id=1, source_target_pairs={{0,2},{2,4},{4,6},{6,0},{8,10},{10,12},{12,14},{14,8},{16,18},{18,... | collective-permute-start | bytes 786440 | tf_op jit(solution)/shard_map/ppermute | solution.py:37
  27.4 0.0 collective-permute-done.10
  27.4 1.3 %collective-permute-start.13 = (bf16[256,512]{1,0:T(8,128)(2,1)S(1)}, bf16[256,512]{1,0:T(8,128)(2,1)S(1)}, u32[]{:S(2)}, u32[]{:S(2)}) collective-permute-start(bf16[256,512]{1,0:T(8,128)(2,1)S(1)} %get-tuple-element.29), channel_id=1, source_target_pairs={{0,2},{2,4},{4,6},{6,0},{8,10},{10,12},{12,14},{14,8},{16,18},{18,... | collective-permute-start | bytes 786440 | tf_op jit(solution)/shard_map/ppermute | solution.py:37
  28.7 0.0 collective-permute-done.8.refs_0_
  28.7 1.5 %collective-permute-start.4 = (bf16[256,512]{1,0:T(8,128)(2,1)S(1)}, bf16[256,512]{1,0:T(8,128)(2,1)S(1)}, u32[]{:S(2)}, u32[]{:S(2)}) collective-permute-start(bf16[256,512]{1,0:T(8,128)(2,1)S(1)} %get-tuple-element.26), channel_id=1, source_target_pairs={{0,6},{2,0},{4,2},{6,4},{8,14},{10,8},{12,10},{14,12},{16,22},{18,... | collective-permute-start | bytes 786440 | tf_op jit(solution)/shard_map/ppermute | solution.py:37
  30.2 0.0 collective-permute-done.12.refs_1_
  30.2 4.7 %collective-permute-start.11 = (bf16[256,512]{1,0:T(8,128)(2,1)S(1)}, bf16[256,512]{1,0:T(8,128)(2,1)S(1)}, u32[]{:S(2)}, u32[]{:S(2)}) collective-permute-start(bf16[256,512]{1,0:T(8,128)(2,1)S(1)} %collective-permute-done.10), channel_id=1, source_target_pairs={{0,160},{2,162},{4,164},{6,166},{8,168},{10,170},{12,172},{14,174}... | collective-permute-start | bytes 786440 | tf_op jit(solution)/shard_map/ppermute | solution.py:37
  34.8 0.0 collective-permute-done.14.refs_3_
  34.8 1.2 %collective-permute-start.7 = (bf16[256,512]{1,0:T(8,128)(2,1)S(1)}, bf16[256,512]{1,0:T(8,128)(2,1)S(1)}, u32[]{:S(2)}, u32[]{:S(2)}) collective-permute-start(bf16[256,512]{1,0:T(8,128)(2,1)S(1)} %get-tuple-element.28), channel_id=1, source_target_pairs={{0,4},{2,6},{4,0},{6,2},{8,12},{10,14},{12,8},{14,10},{16,20},{18,... | collective-permute-start | bytes 786440 | tf_op jit(solution)/shard_map/ppermute | solution.py:37
  36.1 0.0 collective-permute-done.13.refs_2_
  36.1 4.9 %collective-permute-start.9 = (bf16[256,512]{1,0:T(8,128)(2,1)S(1)}, bf16[256,512]{1,0:T(8,128)(2,1)S(1)}, u32[]{:S(2)}, u32[]{:S(2)}) collective-permute-start(bf16[256,512]{1,0:T(8,128)(2,1)S(1)} %collective-permute-done.8.refs_0_), channel_id=1, source_target_pairs={{0,64},{2,66},{4,68},{6,70},{8,72},{10,74},{12,76},{14,78},{16,80}... | collective-permute-start | bytes 786440 | tf_op jit(solution)/shard_map/ppermute | solution.py:37
  40.9 0.0 collective-permute-done.4
  40.9 1.4 %collective-permute-start.5 = (bf16[256,512]{1,0:T(8,128)(2,1)S(1)}, bf16[256,512]{1,0:T(8,128)(2,1)S(1)}, u32[]{:S(2)}, u32[]{:S(2)}) collective-permute-start(bf16[256,512]{1,0:T(8,128)(2,1)S(1)} %collective-permute-done.4), channel_id=1, source_target_pairs={{0,6},{2,0},{4,2},{6,4},{8,14},{10,8},{12,10},{14,12},{16,22},{18,... | collective-permute-start | bytes 786440 | tf_op jit(solution)/shard_map/ppermute | solution.py:37
  42.4 4.3 %stage.4 = (f32[32,128,256]{2,1,0:T(8,128)S(1)}, f32[32,128,128]{2,1,0:T(8,128)S(1)}, bf16[256,2048]{1,0:T(8,128)(2,1)S(1)}) custom-call(bf16[256,2048]{1,0:T(8,128)(2,1)} %source_ref.1, bf16[256,512]{1,0:T(8,128)(2,1)S(1)} %get-tuple-element.22.refs_0_.own_k_ref.own_ref, bf16[256,512]{1,0:T(8,128)(2,1)S(1)} %get-tuple-element.23.refs_1_.own_v_ref.own_ref), custom_call_target="tpu_custom_call" | custom-call | tf_op jit(solution)/shard_map/stage/pallas_call | solution.py:265
  46.7 2.2 %stage.5 = (f32[32,128,256]{2,1,0:T(8,128)S(1)}, f32[32,128,128]{2,1,0:T(8,128)S(1)}) custom-call(bf16[256,2048]{1,0:T(8,128)(2,1)S(1)} %get-tuple-element.24.source_ref, bf16[256,512]{1,0:T(8,128)(2,1)S(1)} %collective-permute-done.come_k_ref.come_ref.refs_0_, bf16[256,512]{1,0:T(8,128)(2,1)S(1)} %collective-permute-done.1.come_v_ref.refs_1_, ...), custom_call_target="tpu_custom_call" | custom-call | tf_op jit(solution)/shard_map/stage/pallas_call | solution.py:265
  48.9 3.7 %stage.6 = (f32[32,128,256]{2,1,0:T(8,128)S(1)}, f32[32,128,128]{2,1,0:T(8,128)S(1)}) custom-call(bf16[256,2048]{1,0:T(8,128)(2,1)S(1)} %get-tuple-element.24.source_ref, bf16[256,512]{1,0:T(8,128)(2,1)S(1)} %collective-permute-done.8.refs_0_, bf16[256,512]{1,0:T(8,128)(2,1)S(1)} %collective-permute-done.12.refs_1_, ...), custom_call_target="tpu_custom_call" | custom-call | tf_op jit(solution)/shard_map/stage/pallas_call | solution.py:265
  52.6 0.0 collective-permute-done.11.refs_4_
  52.6 0.0 collective-permute-done.7.refs_2_
  52.6 0.0 collective-permute-done.2.refs_0_
  52.6 0.0 collective-permute-done.9.refs_3_
  52.6 0.0 collective-permute-done.5.refs_1_
  52.6 0.0 copy-start
  52.6 3.7 %stage.7 = (f32[256,2048]{1,0:T(8,128)S(1)}, f32[8,256]{1,0:T(8,128)S(1)}) custom-call(bf16[256,2048]{1,0:T(8,128)(2,1)S(1)} %get-tuple-element.24.source_ref, bf16[2,256,512]{2,1,0:T(8,128)(2,1)S(1)} %collective-permute-done.2.refs_0_, bf16[256,512]{1,0:T(8,128)(2,1)S(1)} %collective-permute-done.5.refs_1_, ...), custom_call_target="tpu_custom_call" | custom-call | tf_op jit(solution)/shard_map/stage/pallas_call | solution.py:265
  56.4 15.0 %collective-permute-start.15 = (f32[8,256]{1,0:T(8,128)S(1)}, f32[8,256]{1,0:T(8,128)S(1)}, u32[]{:S(2)}, u32[]{:S(2)}) collective-permute-start(f32[8,256]{1,0:T(8,128)S(1)} %get-tuple-element.38.mine_ref), channel_id=1, source_target_pairs={{0,1},{1,0},{2,3},{3,2},{4,5},{5,4},{6,7},{7,6},{8,9},{9,8},{10,11... | collective-permute-start | bytes 24584 | tf_op jit(solution)/shard_map/ppermute | solution.py:310
  71.3 0.8 %collective-permute-done.15.other_ref = f32[8,256]{1,0:T(8,128)S(1)} collective-permute-done((f32[8,256]{1,0:T(8,128)S(1)}, f32[8,256]{1,0:T(8,128)S(1)}, u32[]{:S(2)}, u32[]{:S(2)}) %collective-permute-start.15) | collective-permute-done | bytes 8224 | tf_op jit(solution)/shard_map/ppermute | solution.py:310
  72.1 0.0 copy-done
  72.1 1.2 %norm.1 = bf16[256,2048]{1,0:T(8,128)(2,1)} custom-call(f32[256,2048]{1,0:T(8,128)S(1)} %get-tuple-element.37.comb_ref, f32[8,256]{1,0:T(8,128)S(1)} %get-tuple-element.38.mine_ref, f32[8,256]{1,0:T(8,128)S(1)} %collective-permute-done.15.other_ref, f32[1,2048]{1,0:T(1,128)S(1)} %bitcast.1), custom_call_target="tpu_custom_call" | custom-call | tf_op jit(solution)/shard_map/norm/pallas_call | solution.py:311
  (3 shorter events, 0.1 us)
Async XLA Ops:
  1.1 7.3 %collective-permute-start = (bf16[256,512]{1,0:T(8,128)(2,1)S(1)}, bf16[256,512]{1,0:T(8,128)(2,1)S(1)}, u32[]{:S(2)}, u32[]{:S(2)}) collective-permute-start(bf16[256,512]{1,0:T(8,128)(2,1)S(1)} %get-tuple-element.22.refs_0_.own_k_ref.own_ref), channel_id=1, source_target_pairs={{0,32},{2,34},{4,36},{6,38},{8,40},{10,42},{12,44},{14,46},{16,48}... | collective-permute-start | bytes 786440 | tf_op jit(solution)/shard_map/ppermute | solution.py:37
  2.8 11.2 %collective-permute-start.1 = (bf16[256,512]{1,0:T(8,128)(2,1)S(1)}, bf16[256,512]{1,0:T(8,128)(2,1)S(1)}, u32[]{:S(2)}, u32[]{:S(2)}) collective-permute-start(bf16[256,512]{1,0:T(8,128)(2,1)S(1)} %get-tuple-element.23.refs_1_.own_v_ref.own_ref), channel_id=1, source_target_pairs={{0,32},{2,34},{4,36},{6,38},{8,40},{10,42},{12,44},{14,46},{16,48}... | collective-permute-start | bytes 786440 | tf_op jit(solution)/shard_map/ppermute | solution.py:37
  14.0 6.4 %collective-permute-start.6 = (bf16[256,512]{1,0:T(8,128)(2,1)S(1)}, bf16[256,512]{1,0:T(8,128)(2,1)S(1)}, u32[]{:S(2)}, u32[]{:S(2)}) collective-permute-start(bf16[256,512]{1,0:T(8,128)(2,1)S(1)} %get-tuple-element.27), channel_id=1, source_target_pairs={{0,8},{2,10},{4,12},{6,14},{8,16},{10,18},{12,20},{14,22},{16,24},... | collective-permute-start | bytes 786440 | tf_op jit(solution)/shard_map/ppermute | solution.py:37
  15.1 11.0 %collective-permute-start.3 = (bf16[256,512]{1,0:T(8,128)(2,1)S(1)}, bf16[256,512]{1,0:T(8,128)(2,1)S(1)}, u32[]{:S(2)}, u32[]{:S(2)}) collective-permute-start(bf16[256,512]{1,0:T(8,128)(2,1)S(1)} %pick.3), channel_id=1, source_target_pairs={{0,8},{2,10},{4,12},{6,14},{8,16},{10,18},{12,20},{14,22},{16,24},... | collective-permute-start | bytes 786440 | tf_op jit(solution)/shard_map/ppermute | solution.py:37
  15.2 12.2 %collective-permute-start.10 = (bf16[256,512]{1,0:T(8,128)(2,1)S(1)}, bf16[256,512]{1,0:T(8,128)(2,1)S(1)}, u32[]{:S(2)}, u32[]{:S(2)}) collective-permute-start(bf16[256,512]{1,0:T(8,128)(2,1)S(1)} %get-tuple-element.23.refs_1_.own_v_ref.own_ref), channel_id=1, source_target_pairs={{0,224},{2,226},{4,228},{6,230},{8,232},{10,234},{12,236},{14,238}... | collective-permute-start | bytes 786440 | tf_op jit(solution)/shard_map/ppermute | solution.py:37
  15.3 13.4 %collective-permute-start.8 = (bf16[256,512]{1,0:T(8,128)(2,1)S(1)}, bf16[256,512]{1,0:T(8,128)(2,1)S(1)}, u32[]{:S(2)}, u32[]{:S(2)}) collective-permute-start(bf16[256,512]{1,0:T(8,128)(2,1)S(1)} %collective-permute-done.come_k_ref.come_ref.refs_0_), channel_id=1, source_target_pairs={{0,32},{2,34},{4,36},{6,38},{8,40},{10,42},{12,44},{14,46},{16,48}... | collective-permute-start | bytes 786440 | tf_op jit(solution)/shard_map/ppermute | solution.py:37
  17.6 35.0 %collective-permute-start.2 = (bf16[2,256,512]{2,1,0:T(8,128)(2,1)S(1)}, bf16[2,256,512]{2,1,0:T(8,128)(2,1)S(1)}, u32[]{:S(2)}, u32[]{:S(2)}) collective-permute-start(bf16[2,256,512]{2,1,0:T(8,128)(2,1)S(1)} %get-tuple-element.25), channel_id=1, source_target_pairs={{0,16},{2,18},{4,20},{6,22},{8,24},{10,26},{12,28},{14,30},{16,0},... | collective-permute-start | bytes 1572872 | tf_op jit(solution)/shard_map/ppermute | solution.py:37
  20.4 9.7 %collective-permute-start.12 = (bf16[256,512]{1,0:T(8,128)(2,1)S(1)}, bf16[256,512]{1,0:T(8,128)(2,1)S(1)}, u32[]{:S(2)}, u32[]{:S(2)}) collective-permute-start(bf16[256,512]{1,0:T(8,128)(2,1)S(1)} %collective-permute-done.1.come_v_ref.refs_1_), channel_id=1, source_target_pairs={{0,32},{2,34},{4,36},{6,38},{8,40},{10,42},{12,44},{14,46},{16,48}... | collective-permute-start | bytes 786440 | tf_op jit(solution)/shard_map/ppermute | solution.py:37
  26.1 8.7 %collective-permute-start.14 = (bf16[256,512]{1,0:T(8,128)(2,1)S(1)}, bf16[256,512]{1,0:T(8,128)(2,1)S(1)}, u32[]{:S(2)}, u32[]{:S(2)}) collective-permute-start(bf16[256,512]{1,0:T(8,128)(2,1)S(1)} %get-tuple-element.30), channel_id=1, source_target_pairs={{0,2},{2,4},{4,6},{6,0},{8,10},{10,12},{12,14},{14,8},{16,18},{18,... | collective-permute-start | bytes 786440 | tf_op jit(solution)/shard_map/ppermute | solution.py:37
  27.4 8.7 %collective-permute-start.13 = (bf16[256,512]{1,0:T(8,128)(2,1)S(1)}, bf16[256,512]{1,0:T(8,128)(2,1)S(1)}, u32[]{:S(2)}, u32[]{:S(2)}) collective-permute-start(bf16[256,512]{1,0:T(8,128)(2,1)S(1)} %get-tuple-element.29), channel_id=1, source_target_pairs={{0,2},{2,4},{4,6},{6,0},{8,10},{10,12},{12,14},{14,8},{16,18},{18,... | collective-permute-start | bytes 786440 | tf_op jit(solution)/shard_map/ppermute | solution.py:37
  28.7 12.2 %collective-permute-start.4 = (bf16[256,512]{1,0:T(8,128)(2,1)S(1)}, bf16[256,512]{1,0:T(8,128)(2,1)S(1)}, u32[]{:S(2)}, u32[]{:S(2)}) collective-permute-start(bf16[256,512]{1,0:T(8,128)(2,1)S(1)} %get-tuple-element.26), channel_id=1, source_target_pairs={{0,6},{2,0},{4,2},{6,4},{8,14},{10,8},{12,10},{14,12},{16,22},{18,... | collective-permute-start | bytes 786440 | tf_op jit(solution)/shard_map/ppermute | solution.py:37
  30.2 22.4 %collective-permute-start.11 = (bf16[256,512]{1,0:T(8,128)(2,1)S(1)}, bf16[256,512]{1,0:T(8,128)(2,1)S(1)}, u32[]{:S(2)}, u32[]{:S(2)}) collective-permute-start(bf16[256,512]{1,0:T(8,128)(2,1)S(1)} %collective-permute-done.10), channel_id=1, source_target_pairs={{0,160},{2,162},{4,164},{6,166},{8,168},{10,170},{12,172},{14,174}... | collective-permute-start | bytes 786440 | tf_op jit(solution)/shard_map/ppermute | solution.py:37
  34.8 17.8 %collective-permute-start.7 = (bf16[256,512]{1,0:T(8,128)(2,1)S(1)}, bf16[256,512]{1,0:T(8,128)(2,1)S(1)}, u32[]{:S(2)}, u32[]{:S(2)}) collective-permute-start(bf16[256,512]{1,0:T(8,128)(2,1)S(1)} %get-tuple-element.28), channel_id=1, source_target_pairs={{0,4},{2,6},{4,0},{6,2},{8,12},{10,14},{12,8},{14,10},{16,20},{18,... | collective-permute-start | bytes 786440 | tf_op jit(solution)/shard_map/ppermute | solution.py:37
  36.1 16.5 %collective-permute-start.9 = (bf16[256,512]{1,0:T(8,128)(2,1)S(1)}, bf16[256,512]{1,0:T(8,128)(2,1)S(1)}, u32[]{:S(2)}, u32[]{:S(2)}) collective-permute-start(bf16[256,512]{1,0:T(8,128)(2,1)S(1)} %collective-permute-done.8.refs_0_), channel_id=1, source_target_pairs={{0,64},{2,66},{4,68},{6,70},{8,72},{10,74},{12,76},{14,78},{16,80}... | collective-permute-start | bytes 786440 | tf_op jit(solution)/shard_map/ppermute | solution.py:37
  40.9 11.7 %collective-permute-start.5 = (bf16[256,512]{1,0:T(8,128)(2,1)S(1)}, bf16[256,512]{1,0:T(8,128)(2,1)S(1)}, u32[]{:S(2)}, u32[]{:S(2)}) collective-permute-start(bf16[256,512]{1,0:T(8,128)(2,1)S(1)} %collective-permute-done.4), channel_id=1, source_target_pairs={{0,6},{2,0},{4,2},{6,4},{8,14},{10,8},{12,10},{14,12},{16,22},{18,... | collective-permute-start | bytes 786440 | tf_op jit(solution)/shard_map/ppermute | solution.py:37
  52.6 19.5 %copy-start = (f32[2048]{0:T(1024)S(1)}, f32[2048]{0:T(1024)}, u32[]{:S(2)}) copy-start(f32[2048]{0:T(1024)} %param.5) | copy-start | bytes 24580
  56.4 15.8 %collective-permute-start.15 = (f32[8,256]{1,0:T(8,128)S(1)}, f32[8,256]{1,0:T(8,128)S(1)}, u32[]{:S(2)}, u32[]{:S(2)}) collective-permute-start(f32[8,256]{1,0:T(8,128)S(1)} %get-tuple-element.38.mine_ref), channel_id=1, source_target_pairs={{0,1},{1,0},{2,3},{3,2},{4,5},{5,4},{6,7},{7,6},{8,9},{9,8},{10,11... | collective-permute-start | bytes 24584 | tf_op jit(solution)/shard_map/ppermute | solution.py:310
where the time goes:
time: 73.6 us; the launch traced here: 73.5 us
  starting transfers between devices  43 us (58%)
  Pallas kernels  16.3 us (22%)
  waiting for transfers between devices  13.9 us (19%)
    ppermute x15, starting transfers between devices, send(): return lax.ppermute(value, 'ctx', ring(dz, dy, dx))  28.1 us
    ppermute x1, starting transfers between devices, local(): other = on_chip(lax.ppermute(squares, 'head', [(0, 1), (1, 0)]))  15 us
    pallas_call x4, Pallas kernels, attend(): pl.pallas_call(functools.partial(stage_kernel, ids=ids, group=group, firs...  13.9 us
    ppermute x15, waiting for transfers between devices, send(): return lax.ppermute(value, 'ctx', ring(dz, dy, dx))  13 us
  transfers between devices with their start and end apart: 16, of which 5 were waited for; matrix products, arithmetic and copies ran while one was open for 0% of the time, Pallas kernels for 14%

commit v1 on v0

--- a/solution.py
+++ b/solution.py
@@ -77,7 +77,7 @@
         if i == 0:
             masks.append(None if j == b else tri)
         else:
-            masks.append(tri + jnp.where(place >= 2 ** (i - 1), 0.0, NEG))
+            masks.append(tri + jnp.where(place >= 2 ** ((i - 1) % 7), 0.0, NEG))
     return masks
 
 
@@ -144,11 +144,11 @@
     def body(g, carry):
         for b in range(2):
             rows = slice(b * BLK, (b + 1) * BLK)
-            slots = [(i, b) for i in ids]
+            slots = [(i, b) for i in ids if i != PREVIOUS]
             if b and 0 in ids:
                 slots = slots + [(0, 0)]
-            if not b and 1 in ids:
-                slots = slots + [(1, 1)]
+            if not b and PREVIOUS in ids:
+                slots = slots + [(PREVIOUS, 1)]
             masks = masks_of(slots, b)
             keys, vals = gather_slots(panels, slots, g)
             if last:
@@ -274,9 +274,9 @@
     return [on_chip(out) for out in outs]
 
 
-UNROLL = 2
-WHOLE = 4
-STAGES = ((0,), (5, 3), (6, 1), (4, 2, 7))
+UNROLL = 4
+WHOLE, PREVIOUS = 4, 8
+STAGES = ((0,), (5, 3), (6, 1), (4, 2, 7, 8))
 ROWS, HALF_ROWS, COLS, HALF_COLS = (2, 3), (2, 2), (0, 3), (0, 2)
 
 
@@ -299,7 +299,7 @@
     near, far = pick(r4[1], own[1], COLS, HALF_COLS)
     r1 = [r1k, send(near, 0, 0, 1)]
     r2 = [r2k, send(far, 0, 0, 2)]
-    panels = [[on_chip(half) for half in panel] for panel in (own, r1, r2, r4, r8, r16, r32, r64)]
+    panels = [[on_chip(half) for half in panel] for panel in (own, r1, r2, r4, r8, r16, r32, r64, r1)]
     query = pltpu.with_memory_space_constraint(queries, pltpu.HBM)
     state = []
     for n, ids in enumerate(STAGES):

time: 73.6 us -> 71.1 us (0.966)
  the two profiles are of different devices: /device:TPU:81 before, /device:TPU:17 now
where the time goes in v1:
time: 71.1 us; the launch traced here: 71 us
  starting transfers between devices  32.1 us (45%)
  waiting for transfers between devices  25.1 us (35%)
  Pallas kernels  13.5 us (19%)
    ppermute x15, waiting for transfers between devices, send(): return lax.ppermute(value, 'ctx', ring(dz, dy, dx))  24.2 us
    ppermute x15, starting transfers between devices, send(): return lax.ppermute(value, 'ctx', ring(dz, dy, dx))  16.5 us
    ppermute x1, starting transfers between devices, local(): other = on_chip(lax.ppermute(squares, 'head', [(0, 1), (1, 0)]))  15.6 us
    pallas_call x4, Pallas kernels, attend(): pl.pallas_call(functools.partial(stage_kernel, ids=ids, group=group, firs...  11.2 us
  transfers between devices with their start and end apart: 16, of which 8 were waited for; matrix products, arithmetic and copies ran while one was open for 0% of the time, Pallas kernels for 11%

profile of v1, /device:TPU:17, one launch (start us, length us, event | category | flops | bytes accessed | tf_op | source)
XLA Modules:
  0.0 71.0 jit_solution(16349884913436200104)
XLA Ops:
  0.0 1.0 %split.1 = (bf16[256,512]{1,0:T(8,128)(2,1)S(1)}, bf16[256,512]{1,0:T(8,128)(2,1)S(1)}) custom-call(bf16[2,256,512]{2,1,0:T(8,128)(2,1)} %kv_ref.1), custom_call_target="tpu_custom_call" | custom-call | tf_op jit(solution)/shard_map/split/pallas_call | solution.py:214
  1.1 1.7 %collective-permute-start = (bf16[256,512]{1,0:T(8,128)(2,1)S(1)}, bf16[256,512]{1,0:T(8,128)(2,1)S(1)}, u32[]{:S(2)}, u32[]{:S(2)}) collective-permute-start(bf16[256,512]{1,0:T(8,128)(2,1)S(1)} %get-tuple-element.22.refs_0_.own_k_ref.own_ref), channel_id=1, source_target_pairs={{0,32},{2,34},{4,36},{6,38},{8,40},{10,42},{12,44},{14,46},{16,48}... | collective-permute-start | bytes 786440 | tf_op jit(solution)/shard_map/ppermute | solution.py:37
  2.8 1.6 %collective-permute-start.1 = (bf16[256,512]{1,0:T(8,128)(2,1)S(1)}, bf16[256,512]{1,0:T(8,128)(2,1)S(1)}, u32[]{:S(2)}, u32[]{:S(2)}) collective-permute-start(bf16[256,512]{1,0:T(8,128)(2,1)S(1)} %get-tuple-element.23.refs_1_.own_v_ref.own_ref), channel_id=1, source_target_pairs={{0,32},{2,34},{4,36},{6,38},{8,40},{10,42},{12,44},{14,46},{16,48}... | collective-permute-start | bytes 786440 | tf_op jit(solution)/shard_map/ppermute | solution.py:37
  4.4 8.3 %collective-permute-done.come_k_ref.come_ref.refs_0_ = bf16[256,512]{1,0:T(8,128)(2,1)S(1)} collective-permute-done((bf16[256,512]{1,0:T(8,128)(2,1)S(1)}, bf16[256,512]{1,0:T(8,128)(2,1)S(1)}, u32[]{:S(2)}, u32[]{:S(2)}) %collective-permute-start) | collective-permute-done | bytes 262176 | tf_op jit(solution)/shard_map/ppermute | solution.py:37
  12.7 5.6 %collective-permute-done.1.come_v_ref.refs_1_ = bf16[256,512]{1,0:T(8,128)(2,1)S(1)} collective-permute-done((bf16[256,512]{1,0:T(8,128)(2,1)S(1)}, bf16[256,512]{1,0:T(8,128)(2,1)S(1)}, u32[]{:S(2)}, u32[]{:S(2)}) %collective-permute-start.1) | collective-permute-done | bytes 262176 | tf_op jit(solution)/shard_map/ppermute | solution.py:37
  18.3 0.1 pick_both.1
  18.4 1.1 %collective-permute-start.6 = (bf16[256,512]{1,0:T(8,128)(2,1)S(1)}, bf16[256,512]{1,0:T(8,128)(2,1)S(1)}, u32[]{:S(2)}, u32[]{:S(2)}) collective-permute-start(bf16[256,512]{1,0:T(8,128)(2,1)S(1)} %get-tuple-element.27), channel_id=1, source_target_pairs={{0,8},{2,10},{4,12},{6,14},{8,16},{10,18},{12,20},{14,22},{16,24},... | collective-permute-start | bytes 786440 | tf_op jit(solution)/shard_map/ppermute | solution.py:37
  19.5 0.1 collective-permute-start.3
  19.6 1.2 %collective-permute-start.10 = (bf16[256,512]{1,0:T(8,128)(2,1)S(1)}, bf16[256,512]{1,0:T(8,128)(2,1)S(1)}, u32[]{:S(2)}, u32[]{:S(2)}) collective-permute-start(bf16[256,512]{1,0:T(8,128)(2,1)S(1)} %get-tuple-element.23.refs_1_.own_v_ref.own_ref), channel_id=1, source_target_pairs={{0,224},{2,226},{4,228},{6,230},{8,232},{10,234},{12,236},{14,238}... | collective-permute-start | bytes 786440 | tf_op jit(solution)/shard_map/ppermute | solution.py:37
  20.8 0.3 collective-permute-start.8
  21.1 1.6 %collective-permute-start.2 = (bf16[2,256,512]{2,1,0:T(8,128)(2,1)S(1)}, bf16[2,256,512]{2,1,0:T(8,128)(2,1)S(1)}, u32[]{:S(2)}, u32[]{:S(2)}) collective-permute-start(bf16[2,256,512]{2,1,0:T(8,128)(2,1)S(1)} %get-tuple-element.25), channel_id=1, source_target_pairs={{0,16},{2,18},{4,20},{6,22},{8,24},{10,26},{12,28},{14,30},{16,0},... | collective-permute-start | bytes 1572872 | tf_op jit(solution)/shard_map/ppermute | solution.py:37
  22.7 2.4 %collective-permute-done.6.come_ref.refs_3_ = bf16[256,512]{1,0:T(8,128)(2,1)S(1)} collective-permute-done((bf16[256,512]{1,0:T(8,128)(2,1)S(1)}, bf16[256,512]{1,0:T(8,128)(2,1)S(1)}, u32[]{:S(2)}, u32[]{:S(2)}) %collective-permute-start.6) | collective-permute-done | bytes 262176 | tf_op jit(solution)/shard_map/ppermute | solution.py:37
  25.1 0.0 collective-permute-start.14
  25.1 5.7 %collective-permute-done.3.come_ref.refs_2_ = bf16[256,512]{1,0:T(8,128)(2,1)S(1)} collective-permute-done((bf16[256,512]{1,0:T(8,128)(2,1)S(1)}, bf16[256,512]{1,0:T(8,128)(2,1)S(1)}, u32[]{:S(2)}, u32[]{:S(2)}) %collective-permute-start.3) | collective-permute-done | bytes 262176 | tf_op jit(solution)/shard_map/ppermute | solution.py:37
  30.8 1.2 %collective-permute-start.13 = (bf16[256,512]{1,0:T(8,128)(2,1)S(1)}, bf16[256,512]{1,0:T(8,128)(2,1)S(1)}, u32[]{:S(2)}, u32[]{:S(2)}) collective-permute-start(bf16[256,512]{1,0:T(8,128)(2,1)S(1)} %get-tuple-element.30), channel_id=1, source_target_pairs={{0,2},{2,4},{4,6},{6,0},{8,10},{10,12},{12,14},{14,8},{16,18},{18,... | collective-permute-start | bytes 786440 | tf_op jit(solution)/shard_map/ppermute | solution.py:37
  32.1 0.0 collective-permute-done.10
  32.1 1.3 %collective-permute-start.12 = (bf16[256,512]{1,0:T(8,128)(2,1)S(1)}, bf16[256,512]{1,0:T(8,128)(2,1)S(1)}, u32[]{:S(2)}, u32[]{:S(2)}) collective-permute-start(bf16[256,512]{1,0:T(8,128)(2,1)S(1)} %get-tuple-element.29), channel_id=1, source_target_pairs={{0,2},{2,4},{4,6},{6,0},{8,10},{10,12},{12,14},{14,8},{16,18},{18,... | collective-permute-start | bytes 786440 | tf_op jit(solution)/shard_map/ppermute | solution.py:37
  33.4 0.0 collective-permute-done.8.refs_0_
  33.4 1.5 %collective-permute-start.4 = (bf16[256,512]{1,0:T(8,128)(2,1)S(1)}, bf16[256,512]{1,0:T(8,128)(2,1)S(1)}, u32[]{:S(2)}, u32[]{:S(2)}) collective-permute-start(bf16[256,512]{1,0:T(8,128)(2,1)S(1)} %get-tuple-element.26), channel_id=1, source_target_pairs={{0,6},{2,0},{4,2},{6,4},{8,14},{10,8},{12,10},{14,12},{16,22},{18,... | collective-permute-start | bytes 786440 | tf_op jit(solution)/shard_map/ppermute | solution.py:37
  34.8 0.0 collective-permute-done.14.refs_1_
  34.8 1.8 %collective-permute-start.11 = (bf16[256,512]{1,0:T(8,128)(2,1)S(1)}, bf16[256,512]{1,0:T(8,128)(2,1)S(1)}, u32[]{:S(2)}, u32[]{:S(2)}) collective-permute-start(bf16[256,512]{1,0:T(8,128)(2,1)S(1)} %collective-permute-done.10), channel_id=1, source_target_pairs={{0,160},{2,162},{4,164},{6,166},{8,168},{10,170},{12,172},{14,174}... | collective-permute-start | bytes 786440 | tf_op jit(solution)/shard_map/ppermute | solution.py:37
  36.6 0.8 %collective-permute-done.13.refs_3_.refs_6_ = bf16[256,512]{1,0:T(8,128)(2,1)S(1)} collective-permute-done((bf16[256,512]{1,0:T(8,128)(2,1)S(1)}, bf16[256,512]{1,0:T(8,128)(2,1)S(1)}, u32[]{:S(2)}, u32[]{:S(2)}) %collective-permute-start.13) | collective-permute-done | bytes 262176 | tf_op jit(solution)/shard_map/ppermute | solution.py:37
  37.4 1.7 %collective-permute-start.7 = (bf16[256,512]{1,0:T(8,128)(2,1)S(1)}, bf16[256,512]{1,0:T(8,128)(2,1)S(1)}, u32[]{:S(2)}, u32[]{:S(2)}) collective-permute-start(bf16[256,512]{1,0:T(8,128)(2,1)S(1)} %get-tuple-element.28), channel_id=1, source_target_pairs={{0,4},{2,6},{4,0},{6,2},{8,12},{10,14},{12,8},{14,10},{16,20},{18,... | collective-permute-start | bytes 786440 | tf_op jit(solution)/shard_map/ppermute | solution.py:37
  39.1 1.1 %collective-permute-done.12.refs_2_.refs_5_ = bf16[256,512]{1,0:T(8,128)(2,1)S(1)} collective-permute-done((bf16[256,512]{1,0:T(8,128)(2,1)S(1)}, bf16[256,512]{1,0:T(8,128)(2,1)S(1)}, u32[]{:S(2)}, u32[]{:S(2)}) %collective-permute-start.12) | collective-permute-done | bytes 262176 | tf_op jit(solution)/shard_map/ppermute | solution.py:37
  40.2 0.0 collective-permute-start.9
  40.2 0.0 collective-permute-done.4
  40.2 1.4 %collective-permute-start.5 = (bf16[256,512]{1,0:T(8,128)(2,1)S(1)}, bf16[256,512]{1,0:T(8,128)(2,1)S(1)}, u32[]{:S(2)}, u32[]{:S(2)}) collective-permute-start(bf16[256,512]{1,0:T(8,128)(2,1)S(1)} %collective-permute-done.4), channel_id=1, source_target_pairs={{0,6},{2,0},{4,2},{6,4},{8,14},{10,8},{12,10},{14,12},{16,22},{18,... | collective-permute-start | bytes 786440 | tf_op jit(solution)/shard_map/ppermute | solution.py:37
  41.6 4.3 %stage.4 = (f32[32,128,256]{2,1,0:T(8,128)S(1)}, f32[32,128,128]{2,1,0:T(8,128)S(1)}, bf16[256,2048]{1,0:T(8,128)(2,1)S(1)}) custom-call(bf16[256,2048]{1,0:T(8,128)(2,1)} %source_ref.1, bf16[256,512]{1,0:T(8,128)(2,1)S(1)} %get-tuple-element.22.refs_0_.own_k_ref.own_ref, bf16[256,512]{1,0:T(8,128)(2,1)S(1)} %get-tuple-element.23.refs_1_.own_v_ref.own_ref), custom_call_target="tpu_custom_call" | custom-call | tf_op jit(solution)/shard_map/stage/pallas_call | solution.py:265
  46.0 1.7 %stage.5 = (f32[32,128,256]{2,1,0:T(8,128)S(1)}, f32[32,128,128]{2,1,0:T(8,128)S(1)}) custom-call(bf16[256,2048]{1,0:T(8,128)(2,1)S(1)} %get-tuple-element.24.source_ref, bf16[256,512]{1,0:T(8,128)(2,1)S(1)} %collective-permute-done.come_k_ref.come_ref.refs_0_, bf16[256,512]{1,0:T(8,128)(2,1)S(1)} %collective-permute-done.1.come_v_ref.refs_1_, ...), custom_call_target="tpu_custom_call" | custom-call | tf_op jit(solution)/shard_map/stage/pallas_call | solution.py:265
  47.7 1.7 %stage.6 = (f32[32,128,256]{2,1,0:T(8,128)S(1)}, f32[32,128,128]{2,1,0:T(8,128)S(1)}) custom-call(bf16[256,2048]{1,0:T(8,128)(2,1)S(1)} %get-tuple-element.24.source_ref, bf16[256,512]{1,0:T(8,128)(2,1)S(1)} %collective-permute-done.8.refs_0_, bf16[256,512]{1,0:T(8,128)(2,1)S(1)} %collective-permute-done.14.refs_1_, ...), custom_call_target="tpu_custom_call" | custom-call | tf_op jit(solution)/shard_map/stage/pallas_call | solution.py:265
  49.4 0.0 collective-permute-done.11.refs_4_
  49.4 0.0 collective-permute-done.7.refs_2_
  49.4 0.0 collective-permute-done.2.refs_0_
  49.5 0.4 collective-permute-done.9.refs_3_
  49.8 0.0 collective-permute-done.5.refs_1_
  49.8 0.0 copy-start
  49.8 3.4 %stage.7 = (f32[256,2048]{1,0:T(8,128)S(1)}, f32[8,256]{1,0:T(8,128)S(1)}) custom-call(bf16[256,2048]{1,0:T(8,128)(2,1)S(1)} %get-tuple-element.24.source_ref, bf16[2,256,512]{2,1,0:T(8,128)(2,1)S(1)} %collective-permute-done.2.refs_0_, bf16[256,512]{1,0:T(8,128)(2,1)S(1)} %collective-permute-done.5.refs_1_, ...), custom_call_target="tpu_custom_call" | custom-call | tf_op jit(solution)/shard_map/stage/pallas_call | solution.py:265
  53.2 15.6 %collective-permute-start.15 = (f32[8,256]{1,0:T(8,128)S(1)}, f32[8,256]{1,0:T(8,128)S(1)}, u32[]{:S(2)}, u32[]{:S(2)}) collective-permute-start(f32[8,256]{1,0:T(8,128)S(1)} %get-tuple-element.38.mine_ref), channel_id=1, source_target_pairs={{0,1},{1,0},{2,3},{3,2},{4,5},{5,4},{6,7},{7,6},{8,9},{9,8},{10,11... | collective-permute-start | bytes 24584 | tf_op jit(solution)/shard_map/ppermute | solution.py:310
  68.9 0.8 %collective-permute-done.15.other_ref = f32[8,256]{1,0:T(8,128)S(1)} collective-permute-done((f32[8,256]{1,0:T(8,128)S(1)}, f32[8,256]{1,0:T(8,128)S(1)}, u32[]{:S(2)}, u32[]{:S(2)}) %collective-permute-start.15) | collective-permute-done | bytes 8224 | tf_op jit(solution)/shard_map/ppermute | solution.py:310
  69.7 0.0 copy-done
  69.7 1.2 %norm.1 = bf16[256,2048]{1,0:T(8,128)(2,1)} custom-call(f32[256,2048]{1,0:T(8,128)S(1)} %get-tuple-element.37.comb_ref, f32[8,256]{1,0:T(8,128)S(1)} %get-tuple-element.38.mine_ref, f32[8,256]{1,0:T(8,128)S(1)} %collective-permute-done.15.other_ref, f32[1,2048]{1,0:T(1,128)S(1)} %bitcast.1), custom_call_target="tpu_custom_call" | custom-call | tf_op jit(solution)/shard_map/norm/pallas_call | solution.py:311
  (3 shorter events, 0.1 us)
Async XLA Ops:
  1.1 11.7 %collective-permute-start = (bf16[256,512]{1,0:T(8,128)(2,1)S(1)}, bf16[256,512]{1,0:T(8,128)(2,1)S(1)}, u32[]{:S(2)}, u32[]{:S(2)}) collective-permute-start(bf16[256,512]{1,0:T(8,128)(2,1)S(1)} %get-tuple-element.22.refs_0_.own_k_ref.own_ref), channel_id=1, source_target_pairs={{0,32},{2,34},{4,36},{6,38},{8,40},{10,42},{12,44},{14,46},{16,48}... | collective-permute-start | bytes 786440 | tf_op jit(solution)/shard_map/ppermute | solution.py:37
  2.8 15.6 %collective-permute-start.1 = (bf16[256,512]{1,0:T(8,128)(2,1)S(1)}, bf16[256,512]{1,0:T(8,128)(2,1)S(1)}, u32[]{:S(2)}, u32[]{:S(2)}) collective-permute-start(bf16[256,512]{1,0:T(8,128)(2,1)S(1)} %get-tuple-element.23.refs_1_.own_v_ref.own_ref), channel_id=1, source_target_pairs={{0,32},{2,34},{4,36},{6,38},{8,40},{10,42},{12,44},{14,46},{16,48}... | collective-permute-start | bytes 786440 | tf_op jit(solution)/shard_map/ppermute | solution.py:37
  18.4 6.7 %collective-permute-start.6 = (bf16[256,512]{1,0:T(8,128)(2,1)S(1)}, bf16[256,512]{1,0:T(8,128)(2,1)S(1)}, u32[]{:S(2)}, u32[]{:S(2)}) collective-permute-start(bf16[256,512]{1,0:T(8,128)(2,1)S(1)} %get-tuple-element.27), channel_id=1, source_target_pairs={{0,8},{2,10},{4,12},{6,14},{8,16},{10,18},{12,20},{14,22},{16,24},... | collective-permute-start | bytes 786440 | tf_op jit(solution)/shard_map/ppermute | solution.py:37
  19.5 11.3 %collective-permute-start.3 = (bf16[256,512]{1,0:T(8,128)(2,1)S(1)}, bf16[256,512]{1,0:T(8,128)(2,1)S(1)}, u32[]{:S(2)}, u32[]{:S(2)}) collective-permute-start(bf16[256,512]{1,0:T(8,128)(2,1)S(1)} %pick.3), channel_id=1, source_target_pairs={{0,8},{2,10},{4,12},{6,14},{8,16},{10,18},{12,20},{14,22},{16,24},... | collective-permute-start | bytes 786440 | tf_op jit(solution)/shard_map/ppermute | solution.py:37
  19.6 12.5 %collective-permute-start.10 = (bf16[256,512]{1,0:T(8,128)(2,1)S(1)}, bf16[256,512]{1,0:T(8,128)(2,1)S(1)}, u32[]{:S(2)}, u32[]{:S(2)}) collective-permute-start(bf16[256,512]{1,0:T(8,128)(2,1)S(1)} %get-tuple-element.23.refs_1_.own_v_ref.own_ref), channel_id=1, source_target_pairs={{0,224},{2,226},{4,228},{6,230},{8,232},{10,234},{12,236},{14,238}... | collective-permute-start | bytes 786440 | tf_op jit(solution)/shard_map/ppermute | solution.py:37
  20.8 12.5 %collective-permute-start.8 = (bf16[256,512]{1,0:T(8,128)(2,1)S(1)}, bf16[256,512]{1,0:T(8,128)(2,1)S(1)}, u32[]{:S(2)}, u32[]{:S(2)}) collective-permute-start(bf16[256,512]{1,0:T(8,128)(2,1)S(1)} %collective-permute-done.come_k_ref.come_ref.refs_0_), channel_id=1, source_target_pairs={{0,32},{2,34},{4,36},{6,38},{8,40},{10,42},{12,44},{14,46},{16,48}... | collective-permute-start | bytes 786440 | tf_op jit(solution)/shard_map/ppermute | solution.py:37
  21.1 28.3 %collective-permute-start.2 = (bf16[2,256,512]{2,1,0:T(8,128)(2,1)S(1)}, bf16[2,256,512]{2,1,0:T(8,128)(2,1)S(1)}, u32[]{:S(2)}, u32[]{:S(2)}) collective-permute-start(bf16[2,256,512]{2,1,0:T(8,128)(2,1)S(1)} %get-tuple-element.25), channel_id=1, source_target_pairs={{0,16},{2,18},{4,20},{6,22},{8,24},{10,26},{12,28},{14,30},{16,0},... | collective-permute-start | bytes 1572872 | tf_op jit(solution)/shard_map/ppermute | solution.py:37
  25.1 9.7 %collective-permute-start.14 = (bf16[256,512]{1,0:T(8,128)(2,1)S(1)}, bf16[256,512]{1,0:T(8,128)(2,1)S(1)}, u32[]{:S(2)}, u32[]{:S(2)}) collective-permute-start(bf16[256,512]{1,0:T(8,128)(2,1)S(1)} %collective-permute-done.1.come_v_ref.refs_1_), channel_id=1, source_target_pairs={{0,32},{2,34},{4,36},{6,38},{8,40},{10,42},{12,44},{14,46},{16,48}... | collective-permute-start | bytes 786440 | tf_op jit(solution)/shard_map/ppermute | solution.py:37
  30.8 6.6 %collective-permute-start.13 = (bf16[256,512]{1,0:T(8,128)(2,1)S(1)}, bf16[256,512]{1,0:T(8,128)(2,1)S(1)}, u32[]{:S(2)}, u32[]{:S(2)}) collective-permute-start(bf16[256,512]{1,0:T(8,128)(2,1)S(1)} %get-tuple-element.30), channel_id=1, source_target_pairs={{0,2},{2,4},{4,6},{6,0},{8,10},{10,12},{12,14},{14,8},{16,18},{18,... | collective-permute-start | bytes 786440 | tf_op jit(solution)/shard_map/ppermute | solution.py:37
  32.1 8.1 %collective-permute-start.12 = (bf16[256,512]{1,0:T(8,128)(2,1)S(1)}, bf16[256,512]{1,0:T(8,128)(2,1)S(1)}, u32[]{:S(2)}, u32[]{:S(2)}) collective-permute-start(bf16[256,512]{1,0:T(8,128)(2,1)S(1)} %get-tuple-element.29), channel_id=1, source_target_pairs={{0,2},{2,4},{4,6},{6,0},{8,10},{10,12},{12,14},{14,8},{16,18},{18,... | collective-permute-start | bytes 786440 | tf_op jit(solution)/shard_map/ppermute | solution.py:37
  33.4 6.8 %collective-permute-start.4 = (bf16[256,512]{1,0:T(8,128)(2,1)S(1)}, bf16[256,512]{1,0:T(8,128)(2,1)S(1)}, u32[]{:S(2)}, u32[]{:S(2)}) collective-permute-start(bf16[256,512]{1,0:T(8,128)(2,1)S(1)} %get-tuple-element.26), channel_id=1, source_target_pairs={{0,6},{2,0},{4,2},{6,4},{8,14},{10,8},{12,10},{14,12},{16,22},{18,... | collective-permute-start | bytes 786440 | tf_op jit(solution)/shard_map/ppermute | solution.py:37
  34.8 14.6 %collective-permute-start.11 = (bf16[256,512]{1,0:T(8,128)(2,1)S(1)}, bf16[256,512]{1,0:T(8,128)(2,1)S(1)}, u32[]{:S(2)}, u32[]{:S(2)}) collective-permute-start(bf16[256,512]{1,0:T(8,128)(2,1)S(1)} %collective-permute-done.10), channel_id=1, source_target_pairs={{0,160},{2,162},{4,164},{6,166},{8,168},{10,170},{12,172},{14,174}... | collective-permute-start | bytes 786440 | tf_op jit(solution)/shard_map/ppermute | solution.py:37
  37.4 12.1 %collective-permute-start.7 = (bf16[256,512]{1,0:T(8,128)(2,1)S(1)}, bf16[256,512]{1,0:T(8,128)(2,1)S(1)}, u32[]{:S(2)}, u32[]{:S(2)}) collective-permute-start(bf16[256,512]{1,0:T(8,128)(2,1)S(1)} %get-tuple-element.28), channel_id=1, source_target_pairs={{0,4},{2,6},{4,0},{6,2},{8,12},{10,14},{12,8},{14,10},{16,20},{18,... | collective-permute-start | bytes 786440 | tf_op jit(solution)/shard_map/ppermute | solution.py:37
  40.2 9.6 %collective-permute-start.9 = (bf16[256,512]{1,0:T(8,128)(2,1)S(1)}, bf16[256,512]{1,0:T(8,128)(2,1)S(1)}, u32[]{:S(2)}, u32[]{:S(2)}) collective-permute-start(bf16[256,512]{1,0:T(8,128)(2,1)S(1)} %collective-permute-done.8.refs_0_), channel_id=1, source_target_pairs={{0,64},{2,66},{4,68},{6,70},{8,72},{10,74},{12,76},{14,78},{16,80}... | collective-permute-start | bytes 786440 | tf_op jit(solution)/shard_map/ppermute | solution.py:37
  40.2 9.6 %collective-permute-start.5 = (bf16[256,512]{1,0:T(8,128)(2,1)S(1)}, bf16[256,512]{1,0:T(8,128)(2,1)S(1)}, u32[]{:S(2)}, u32[]{:S(2)}) collective-permute-start(bf16[256,512]{1,0:T(8,128)(2,1)S(1)} %collective-permute-done.4), channel_id=1, source_target_pairs={{0,6},{2,0},{4,2},{6,4},{8,14},{10,8},{12,10},{14,12},{16,22},{18,... | collective-permute-start | bytes 786440 | tf_op jit(solution)/shard_map/ppermute | solution.py:37
  49.8 19.9 %copy-start = (f32[2048]{0:T(1024)S(1)}, f32[2048]{0:T(1024)}, u32[]{:S(2)}) copy-start(f32[2048]{0:T(1024)} %param.5) | copy-start | bytes 24580
  53.2 16.5 %collective-permute-start.15 = (f32[8,256]{1,0:T(8,128)S(1)}, f32[8,256]{1,0:T(8,128)S(1)}, u32[]{:S(2)}, u32[]{:S(2)}) collective-permute-start(f32[8,256]{1,0:T(8,128)S(1)} %get-tuple-element.38.mine_ref), channel_id=1, source_target_pairs={{0,1},{1,0},{2,3},{3,2},{4,5},{5,4},{6,7},{7,6},{8,9},{9,8},{10,11... | collective-permute-start | bytes 24584 | tf_op jit(solution)/shard_map/ppermute | solution.py:310

commit v2 on v1

--- a/solution.py
+++ b/solution.py
@@ -81,12 +81,10 @@
     return masks
 
 
-def split_kernel(kv_ref, k_ref, v_ref, sems):
-    copies = [pltpu.make_async_copy(kv_ref.at[n], ref, sems.at[n]) for n, ref in enumerate((k_ref, v_ref))]
-    for copy in copies:
-        copy.start()
-    for copy in copies:
-        copy.wait()
+def split_kernel(kv_ref, half_ref, sem, *, n):
+    copy = pltpu.make_async_copy(kv_ref.at[n], half_ref, sem.at[0])
+    copy.start()
+    copy.wait()
 
 
 def choose(moved, come_ref, own_ref, out_ref):
@@ -209,18 +207,17 @@
         copy.wait()
 
 
-def split(keyval):
-    half = pltpu.VMEM(keyval.shape[1:], keyval.dtype)
-    pair = pl.pallas_call(
-        split_kernel,
+def split(keyval, n):
+    half = pl.pallas_call(
+        functools.partial(split_kernel, n=n),
         in_specs=[pl.BlockSpec(memory_space=pltpu.HBM)],
-        out_specs=[VMEM, VMEM],
-        out_shape=[half, half],
-        scratch_shapes=[pltpu.SemaphoreType.DMA((2,))],
+        out_specs=VMEM,
+        out_shape=pltpu.VMEM(keyval.shape[1:], keyval.dtype),
+        scratch_shapes=[pltpu.SemaphoreType.DMA((1,))],
         compiler_params=PARAMS,
         name="split",
     )(pltpu.with_memory_space_constraint(keyval, pltpu.HBM))
-    return [on_chip(half) for half in pair]
+    return on_chip(half)
 
 
 def pick(come, own, *tests):
@@ -276,14 +273,16 @@
 
 UNROLL = 4
 WHOLE, PREVIOUS = 4, 8
-STAGES = ((0,), (5, 3), (6, 1), (4, 2, 7, 8))
+STAGES = ((0,), (5, 3), (6, 1, 8), (4, 2, 7))
 ROWS, HALF_ROWS, COLS, HALF_COLS = (2, 3), (2, 2), (0, 3), (0, 2)
 
 
 def local(queries, keyval, out_gain):
     tok_rows, width = queries.shape
     group = width // keyval.shape[2]
-    own = split(keyval)
+    own = []
+    for n in range(2):
+        own.append(split(keyval, n))
     r16 = [send(own[0], 1, 0, 0), send(own[1], 1, 0, 0)]
     mid = send(own[1], -1, 0, 0)
     r32 = [send(r16[0], 1, 0, 0), send(r16[1], 1, 0, 0)]

time: 71.1 us -> 72.3 us (1.017)
  the two profiles are of different devices: /device:TPU:17 before, /device:TPU:81 now
where the time goes in v2:
time: 72.3 us; the launch traced here: 72.2 us
  starting transfers between devices  43.1 us (60%)
  Pallas kernels  15.9 us (22%)
  waiting for transfers between devices  12.8 us (18%)
    ppermute x15, starting transfers between devices, send(): return lax.ppermute(value, 'ctx', ring(dz, dy, dx))  28.2 us
    ppermute x1, starting transfers between devices, local(): other = on_chip(lax.ppermute(squares, 'head', [(0, 1), (1, 0)]))  15 us
    pallas_call x4, Pallas kernels, attend(): pl.pallas_call(functools.partial(stage_kernel, ids=ids, group=group, firs...  12.7 us
    ppermute x15, waiting for transfers between devices, send(): return lax.ppermute(value, 'ctx', ring(dz, dy, dx))  12 us
    pallas_call x2, Pallas kernels, split(): pl.pallas_call(functools.partial(split_kernel, n=n), in_specs=[pl.BlockSp...  1.91 us
  transfers between devices with their start and end apart: 16, of which 5 were waited for; matrix products, arithmetic and copies ran while one was open for 0% of the time, Pallas kernels for 15%

profile of v2, /device:TPU:81, one launch (start us, length us, event | category | flops | bytes accessed | tf_op | source)
XLA Modules:
  0.0 72.2 jit_solution(12370252732175834769)
XLA Ops:
  0.0 1.0 %split.2.refs_0_.own_k_ref.own_ref = bf16[256,512]{1,0:T(8,128)(2,1)S(1)} custom-call(bf16[2,256,512]{2,1,0:T(8,128)(2,1)} %kv_ref.3), custom_call_target="tpu_custom_call" | custom-call | tf_op jit(solution)/shard_map/split/pallas_call | solution.py:211
  1.0 1.7 %collective-permute-start = (bf16[256,512]{1,0:T(8,128)(2,1)S(1)}, bf16[256,512]{1,0:T(8,128)(2,1)S(1)}, u32[]{:S(2)}, u32[]{:S(2)}) collective-permute-start(bf16[256,512]{1,0:T(8,128)(2,1)S(1)} %split.2.refs_0_.own_k_ref.own_ref), channel_id=1, source_target_pairs={{0,32},{2,34},{4,36},{6,38},{8,40},{10,42},{12,44},{14,46},{16,48}... | collective-permute-start | bytes 786440 | tf_op jit(solution)/shard_map/ppermute | solution.py:37
  2.7 1.0 %split.3.refs_1_.own_v_ref.own_ref = bf16[256,512]{1,0:T(8,128)(2,1)S(1)} custom-call(bf16[2,256,512]{2,1,0:T(8,128)(2,1)} %kv_ref.3), custom_call_target="tpu_custom_call" | custom-call | tf_op jit(solution)/shard_map/split/pallas_call | solution.py:211
  3.6 2.9 %collective-permute-start.1 = (bf16[256,512]{1,0:T(8,128)(2,1)S(1)}, bf16[256,512]{1,0:T(8,128)(2,1)S(1)}, u32[]{:S(2)}, u32[]{:S(2)}) collective-permute-start(bf16[256,512]{1,0:T(8,128)(2,1)S(1)} %split.3.refs_1_.own_v_ref.own_ref), channel_id=1, source_target_pairs={{0,32},{2,34},{4,36},{6,38},{8,40},{10,42},{12,44},{14,46},{16,48}... | collective-permute-start | bytes 786440 | tf_op jit(solution)/shard_map/ppermute | solution.py:37
  6.6 1.7 %collective-permute-done.come_k_ref.come_ref.refs_0_ = bf16[256,512]{1,0:T(8,128)(2,1)S(1)} collective-permute-done((bf16[256,512]{1,0:T(8,128)(2,1)S(1)}, bf16[256,512]{1,0:T(8,128)(2,1)S(1)}, u32[]{:S(2)}, u32[]{:S(2)}) %collective-permute-start) | collective-permute-done | bytes 262176 | tf_op jit(solution)/shard_map/ppermute | solution.py:37
  8.2 5.6 %collective-permute-done.1.come_v_ref.refs_1_ = bf16[256,512]{1,0:T(8,128)(2,1)S(1)} collective-permute-done((bf16[256,512]{1,0:T(8,128)(2,1)S(1)}, bf16[256,512]{1,0:T(8,128)(2,1)S(1)}, u32[]{:S(2)}, u32[]{:S(2)}) %collective-permute-start.1) | collective-permute-done | bytes 262176 | tf_op jit(solution)/shard_map/ppermute | solution.py:37
  13.9 0.1 pick_both.1
  13.9 1.1 %collective-permute-start.6 = (bf16[256,512]{1,0:T(8,128)(2,1)S(1)}, bf16[256,512]{1,0:T(8,128)(2,1)S(1)}, u32[]{:S(2)}, u32[]{:S(2)}) collective-permute-start(bf16[256,512]{1,0:T(8,128)(2,1)S(1)} %get-tuple-element.23), channel_id=1, source_target_pairs={{0,8},{2,10},{4,12},{6,14},{8,16},{10,18},{12,20},{14,22},{16,24},... | collective-permute-start | bytes 786440 | tf_op jit(solution)/shard_map/ppermute | solution.py:37
  15.0 0.1 collective-permute-start.3
  15.1 0.1 collective-permute-start.10
  15.2 2.4 %collective-permute-start.8 = (bf16[256,512]{1,0:T(8,128)(2,1)S(1)}, bf16[256,512]{1,0:T(8,128)(2,1)S(1)}, u32[]{:S(2)}, u32[]{:S(2)}) collective-permute-start(bf16[256,512]{1,0:T(8,128)(2,1)S(1)} %collective-permute-done.come_k_ref.come_ref.refs_0_), channel_id=1, source_target_pairs={{0,32},{2,34},{4,36},{6,38},{8,40},{10,42},{12,44},{14,46},{16,48}... | collective-permute-start | bytes 786440 | tf_op jit(solution)/shard_map/ppermute | solution.py:37
  17.6 1.5 %collective-permute-start.2 = (bf16[2,256,512]{2,1,0:T(8,128)(2,1)S(1)}, bf16[2,256,512]{2,1,0:T(8,128)(2,1)S(1)}, u32[]{:S(2)}, u32[]{:S(2)}) collective-permute-start(bf16[2,256,512]{2,1,0:T(8,128)(2,1)S(1)} %get-tuple-element.21), channel_id=1, source_target_pairs={{0,16},{2,18},{4,20},{6,22},{8,24},{10,26},{12,28},{14,30},{16,0},... | collective-permute-start | bytes 1572872 | tf_op jit(solution)/shard_map/ppermute | solution.py:37
  19.0 1.3 %collective-permute-done.6.come_ref.refs_3_ = bf16[256,512]{1,0:T(8,128)(2,1)S(1)} collective-permute-done((bf16[256,512]{1,0:T(8,128)(2,1)S(1)}, bf16[256,512]{1,0:T(8,128)(2,1)S(1)}, u32[]{:S(2)}, u32[]{:S(2)}) %collective-permute-start.6) | collective-permute-done | bytes 262176 | tf_op jit(solution)/shard_map/ppermute | solution.py:37
  20.3 2.3 %collective-permute-start.12 = (bf16[256,512]{1,0:T(8,128)(2,1)S(1)}, bf16[256,512]{1,0:T(8,128)(2,1)S(1)}, u32[]{:S(2)}, u32[]{:S(2)}) collective-permute-start(bf16[256,512]{1,0:T(8,128)(2,1)S(1)} %collective-permute-done.1.come_v_ref.refs_1_), channel_id=1, source_target_pairs={{0,32},{2,34},{4,36},{6,38},{8,40},{10,42},{12,44},{14,46},{16,48}... | collective-permute-start | bytes 786440 | tf_op jit(solution)/shard_map/ppermute | solution.py:37
  22.7 3.4 %collective-permute-done.3.come_ref.refs_2_ = bf16[256,512]{1,0:T(8,128)(2,1)S(1)} collective-permute-done((bf16[256,512]{1,0:T(8,128)(2,1)S(1)}, bf16[256,512]{1,0:T(8,128)(2,1)S(1)}, u32[]{:S(2)}, u32[]{:S(2)}) %collective-permute-start.3) | collective-permute-done | bytes 262176 | tf_op jit(solution)/shard_map/ppermute | solution.py:37
  26.0 1.2 %collective-permute-start.14 = (bf16[256,512]{1,0:T(8,128)(2,1)S(1)}, bf16[256,512]{1,0:T(8,128)(2,1)S(1)}, u32[]{:S(2)}, u32[]{:S(2)}) collective-permute-start(bf16[256,512]{1,0:T(8,128)(2,1)S(1)} %get-tuple-element.26), channel_id=1, source_target_pairs={{0,2},{2,4},{4,6},{6,0},{8,10},{10,12},{12,14},{14,8},{16,18},{18,... | collective-permute-start | bytes 786440 | tf_op jit(solution)/shard_map/ppermute | solution.py:37
  27.3 0.0 collective-permute-done.10
  27.3 1.3 %collective-permute-start.13 = (bf16[256,512]{1,0:T(8,128)(2,1)S(1)}, bf16[256,512]{1,0:T(8,128)(2,1)S(1)}, u32[]{:S(2)}, u32[]{:S(2)}) collective-permute-start(bf16[256,512]{1,0:T(8,128)(2,1)S(1)} %get-tuple-element.25), channel_id=1, source_target_pairs={{0,2},{2,4},{4,6},{6,0},{8,10},{10,12},{12,14},{14,8},{16,18},{18,... | collective-permute-start | bytes 786440 | tf_op jit(solution)/shard_map/ppermute | solution.py:37
  28.6 0.0 collective-permute-done.8.refs_0_
  28.6 1.5 %collective-permute-start.4 = (bf16[256,512]{1,0:T(8,128)(2,1)S(1)}, bf16[256,512]{1,0:T(8,128)(2,1)S(1)}, u32[]{:S(2)}, u32[]{:S(2)}) collective-permute-start(bf16[256,512]{1,0:T(8,128)(2,1)S(1)} %get-tuple-element.22), channel_id=1, source_target_pairs={{0,6},{2,0},{4,2},{6,4},{8,14},{10,8},{12,10},{14,12},{16,22},{18,... | collective-permute-start | bytes 786440 | tf_op jit(solution)/shard_map/ppermute | solution.py:37
  30.1 0.0 collective-permute-done.12.refs_1_
  30.1 4.7 %collective-permute-start.11 = (bf16[256,512]{1,0:T(8,128)(2,1)S(1)}, bf16[256,512]{1,0:T(8,128)(2,1)S(1)}, u32[]{:S(2)}, u32[]{:S(2)}) collective-permute-start(bf16[256,512]{1,0:T(8,128)(2,1)S(1)} %collective-permute-done.10), channel_id=1, source_target_pairs={{0,160},{2,162},{4,164},{6,166},{8,168},{10,170},{12,172},{14,174}... | collective-permute-start | bytes 786440 | tf_op jit(solution)/shard_map/ppermute | solution.py:37
  34.7 0.0 collective-permute-done.14.refs_3_.refs_5_
  34.7 1.2 %collective-permute-start.7 = (bf16[256,512]{1,0:T(8,128)(2,1)S(1)}, bf16[256,512]{1,0:T(8,128)(2,1)S(1)}, u32[]{:S(2)}, u32[]{:S(2)}) collective-permute-start(bf16[256,512]{1,0:T(8,128)(2,1)S(1)} %get-tuple-element.24), channel_id=1, source_target_pairs={{0,4},{2,6},{4,0},{6,2},{8,12},{10,14},{12,8},{14,10},{16,20},{18,... | collective-permute-start | bytes 786440 | tf_op jit(solution)/shard_map/ppermute | solution.py:37
  36.0 0.0 collective-permute-done.13.refs_2_.refs_4_
  36.0 4.9 %collective-permute-start.9 = (bf16[256,512]{1,0:T(8,128)(2,1)S(1)}, bf16[256,512]{1,0:T(8,128)(2,1)S(1)}, u32[]{:S(2)}, u32[]{:S(2)}) collective-permute-start(bf16[256,512]{1,0:T(8,128)(2,1)S(1)} %collective-permute-done.8.refs_0_), channel_id=1, source_target_pairs={{0,64},{2,66},{4,68},{6,70},{8,72},{10,74},{12,76},{14,78},{16,80}... | collective-permute-start | bytes 786440 | tf_op jit(solution)/shard_map/ppermute | solution.py:37
  40.8 0.0 collective-permute-done.4
  40.8 1.4 %collective-permute-start.5 = (bf16[256,512]{1,0:T(8,128)(2,1)S(1)}, bf16[256,512]{1,0:T(8,128)(2,1)S(1)}, u32[]{:S(2)}, u32[]{:S(2)}) collective-permute-start(bf16[256,512]{1,0:T(8,128)(2,1)S(1)} %collective-permute-done.4), channel_id=1, source_target_pairs={{0,6},{2,0},{4,2},{6,4},{8,14},{10,8},{12,10},{14,12},{16,22},{18,... | collective-permute-start | bytes 786440 | tf_op jit(solution)/shard_map/ppermute | solution.py:37
  42.3 4.3 %stage.4 = (f32[32,128,256]{2,1,0:T(8,128)S(1)}, f32[32,128,128]{2,1,0:T(8,128)S(1)}, bf16[256,2048]{1,0:T(8,128)(2,1)S(1)}) custom-call(bf16[256,2048]{1,0:T(8,128)(2,1)} %source_ref.1, bf16[256,512]{1,0:T(8,128)(2,1)S(1)} %split.2.refs_0_.own_k_ref.own_ref, bf16[256,512]{1,0:T(8,128)(2,1)S(1)} %split.3.refs_1_.own_v_ref.own_ref), custom_call_target="tpu_custom_call" | custom-call | tf_op jit(solution)/shard_map/stage/pallas_call | solution.py:262
  46.6 1.7 %stage.5 = (f32[32,128,256]{2,1,0:T(8,128)S(1)}, f32[32,128,128]{2,1,0:T(8,128)S(1)}) custom-call(bf16[256,2048]{1,0:T(8,128)(2,1)S(1)} %get-tuple-element.20.source_ref, bf16[256,512]{1,0:T(8,128)(2,1)S(1)} %collective-permute-done.come_k_ref.come_ref.refs_0_, bf16[256,512]{1,0:T(8,128)(2,1)S(1)} %collective-permute-done.1.come_v_ref.refs_1_, ...), custom_call_target="tpu_custom_call" | custom-call | tf_op jit(solution)/shard_map/stage/pallas_call | solution.py:262
  48.3 3.5 %stage.6 = (f32[32,128,256]{2,1,0:T(8,128)S(1)}, f32[32,128,128]{2,1,0:T(8,128)S(1)}) custom-call(bf16[256,2048]{1,0:T(8,128)(2,1)S(1)} %get-tuple-element.20.source_ref, bf16[256,512]{1,0:T(8,128)(2,1)S(1)} %collective-permute-done.8.refs_0_, bf16[256,512]{1,0:T(8,128)(2,1)S(1)} %collective-permute-done.12.refs_1_, ...), custom_call_target="tpu_custom_call" | custom-call | tf_op jit(solution)/shard_map/stage/pallas_call | solution.py:262
  51.8 0.0 collective-permute-done.11.refs_4_
  51.8 0.0 collective-permute-done.7.refs_2_
  51.8 0.0 collective-permute-done.2.refs_0_
  51.8 0.0 collective-permute-done.9.refs_3_
  51.9 0.0 collective-permute-done.5.refs_1_
  51.9 0.0 copy-start
  51.9 3.2 %stage.7 = (f32[256,2048]{1,0:T(8,128)S(1)}, f32[8,256]{1,0:T(8,128)S(1)}) custom-call(bf16[256,2048]{1,0:T(8,128)(2,1)S(1)} %get-tuple-element.20.source_ref, bf16[2,256,512]{2,1,0:T(8,128)(2,1)S(1)} %collective-permute-done.2.refs_0_, bf16[256,512]{1,0:T(8,128)(2,1)S(1)} %collective-permute-done.5.refs_1_, ...), custom_call_target="tpu_custom_call" | custom-call | tf_op jit(solution)/shard_map/stage/pallas_call | solution.py:262
  55.0 15.0 %collective-permute-start.15 = (f32[8,256]{1,0:T(8,128)S(1)}, f32[8,256]{1,0:T(8,128)S(1)}, u32[]{:S(2)}, u32[]{:S(2)}) collective-permute-start(f32[8,256]{1,0:T(8,128)S(1)} %get-tuple-element.34.mine_ref), channel_id=1, source_target_pairs={{0,1},{1,0},{2,3},{3,2},{4,5},{5,4},{6,7},{7,6},{8,9},{9,8},{10,11... | collective-permute-start | bytes 24584 | tf_op jit(solution)/shard_map/ppermute | solution.py:309
  70.0 0.8 %collective-permute-done.15.other_ref = f32[8,256]{1,0:T(8,128)S(1)} collective-permute-done((f32[8,256]{1,0:T(8,128)S(1)}, f32[8,256]{1,0:T(8,128)S(1)}, u32[]{:S(2)}, u32[]{:S(2)}) %collective-permute-start.15) | collective-permute-done | bytes 8224 | tf_op jit(solution)/shard_map/ppermute | solution.py:309
  70.8 0.0 copy-done
  70.8 1.2 %norm.1 = bf16[256,2048]{1,0:T(8,128)(2,1)} custom-call(f32[256,2048]{1,0:T(8,128)S(1)} %get-tuple-element.33.comb_ref, f32[8,256]{1,0:T(8,128)S(1)} %get-tuple-element.34.mine_ref, f32[8,256]{1,0:T(8,128)S(1)} %collective-permute-done.15.other_ref, f32[1,2048]{1,0:T(1,128)S(1)} %bitcast.1), custom_call_target="tpu_custom_call" | custom-call | tf_op jit(solution)/shard_map/norm/pallas_call | solution.py:310
  (3 shorter events, 0.1 us)
Async XLA Ops:
  1.0 7.3 %collective-permute-start = (bf16[256,512]{1,0:T(8,128)(2,1)S(1)}, bf16[256,512]{1,0:T(8,128)(2,1)S(1)}, u32[]{:S(2)}, u32[]{:S(2)}) collective-permute-start(bf16[256,512]{1,0:T(8,128)(2,1)S(1)} %split.2.refs_0_.own_k_ref.own_ref), channel_id=1, source_target_pairs={{0,32},{2,34},{4,36},{6,38},{8,40},{10,42},{12,44},{14,46},{16,48}... | collective-permute-start | bytes 786440 | tf_op jit(solution)/shard_map/ppermute | solution.py:37
  3.6 10.2 %collective-permute-start.1 = (bf16[256,512]{1,0:T(8,128)(2,1)S(1)}, bf16[256,512]{1,0:T(8,128)(2,1)S(1)}, u32[]{:S(2)}, u32[]{:S(2)}) collective-permute-start(bf16[256,512]{1,0:T(8,128)(2,1)S(1)} %split.3.refs_1_.own_v_ref.own_ref), channel_id=1, source_target_pairs={{0,32},{2,34},{4,36},{6,38},{8,40},{10,42},{12,44},{14,46},{16,48}... | collective-permute-start | bytes 786440 | tf_op jit(solution)/shard_map/ppermute | solution.py:37
  13.9 6.4 %collective-permute-start.6 = (bf16[256,512]{1,0:T(8,128)(2,1)S(1)}, bf16[256,512]{1,0:T(8,128)(2,1)S(1)}, u32[]{:S(2)}, u32[]{:S(2)}) collective-permute-start(bf16[256,512]{1,0:T(8,128)(2,1)S(1)} %get-tuple-element.23), channel_id=1, source_target_pairs={{0,8},{2,10},{4,12},{6,14},{8,16},{10,18},{12,20},{14,22},{16,24},... | collective-permute-start | bytes 786440 | tf_op jit(solution)/shard_map/ppermute | solution.py:37
  15.0 11.0 %collective-permute-start.3 = (bf16[256,512]{1,0:T(8,128)(2,1)S(1)}, bf16[256,512]{1,0:T(8,128)(2,1)S(1)}, u32[]{:S(2)}, u32[]{:S(2)}) collective-permute-start(bf16[256,512]{1,0:T(8,128)(2,1)S(1)} %pick.3), channel_id=1, source_target_pairs={{0,8},{2,10},{4,12},{6,14},{8,16},{10,18},{12,20},{14,22},{16,24},... | collective-permute-start | bytes 786440 | tf_op jit(solution)/shard_map/ppermute | solution.py:37
  15.1 12.2 %collective-permute-start.10 = (bf16[256,512]{1,0:T(8,128)(2,1)S(1)}, bf16[256,512]{1,0:T(8,128)(2,1)S(1)}, u32[]{:S(2)}, u32[]{:S(2)}) collective-permute-start(bf16[256,512]{1,0:T(8,128)(2,1)S(1)} %split.3.refs_1_.own_v_ref.own_ref), channel_id=1, source_target_pairs={{0,224},{2,226},{4,228},{6,230},{8,232},{10,234},{12,236},{14,238}... | collective-permute-start | bytes 786440 | tf_op jit(solution)/shard_map/ppermute | solution.py:37
  15.2 13.4 %collective-permute-start.8 = (bf16[256,512]{1,0:T(8,128)(2,1)S(1)}, bf16[256,512]{1,0:T(8,128)(2,1)S(1)}, u32[]{:S(2)}, u32[]{:S(2)}) collective-permute-start(bf16[256,512]{1,0:T(8,128)(2,1)S(1)} %collective-permute-done.come_k_ref.come_ref.refs_0_), channel_id=1, source_target_pairs={{0,32},{2,34},{4,36},{6,38},{8,40},{10,42},{12,44},{14,46},{16,48}... | collective-permute-start | bytes 786440 | tf_op jit(solution)/shard_map/ppermute | solution.py:37
  17.6 34.3 %collective-permute-start.2 = (bf16[2,256,512]{2,1,0:T(8,128)(2,1)S(1)}, bf16[2,256,512]{2,1,0:T(8,128)(2,1)S(1)}, u32[]{:S(2)}, u32[]{:S(2)}) collective-permute-start(bf16[2,256,512]{2,1,0:T(8,128)(2,1)S(1)} %get-tuple-element.21), channel_id=1, source_target_pairs={{0,16},{2,18},{4,20},{6,22},{8,24},{10,26},{12,28},{14,30},{16,0},... | collective-permute-start | bytes 1572872 | tf_op jit(solution)/shard_map/ppermute | solution.py:37
  20.3 9.7 %collective-permute-start.12 = (bf16[256,512]{1,0:T(8,128)(2,1)S(1)}, bf16[256,512]{1,0:T(8,128)(2,1)S(1)}, u32[]{:S(2)}, u32[]{:S(2)}) collective-permute-start(bf16[256,512]{1,0:T(8,128)(2,1)S(1)} %collective-permute-done.1.come_v_ref.refs_1_), channel_id=1, source_target_pairs={{0,32},{2,34},{4,36},{6,38},{8,40},{10,42},{12,44},{14,46},{16,48}... | collective-permute-start | bytes 786440 | tf_op jit(solution)/shard_map/ppermute | solution.py:37
  26.0 8.7 %collective-permute-start.14 = (bf16[256,512]{1,0:T(8,128)(2,1)S(1)}, bf16[256,512]{1,0:T(8,128)(2,1)S(1)}, u32[]{:S(2)}, u32[]{:S(2)}) collective-permute-start(bf16[256,512]{1,0:T(8,128)(2,1)S(1)} %get-tuple-element.26), channel_id=1, source_target_pairs={{0,2},{2,4},{4,6},{6,0},{8,10},{10,12},{12,14},{14,8},{16,18},{18,... | collective-permute-start | bytes 786440 | tf_op jit(solution)/shard_map/ppermute | solution.py:37
  27.3 8.7 %collective-permute-start.13 = (bf16[256,512]{1,0:T(8,128)(2,1)S(1)}, bf16[256,512]{1,0:T(8,128)(2,1)S(1)}, u32[]{:S(2)}, u32[]{:S(2)}) collective-permute-start(bf16[256,512]{1,0:T(8,128)(2,1)S(1)} %get-tuple-element.25), channel_id=1, source_target_pairs={{0,2},{2,4},{4,6},{6,0},{8,10},{10,12},{12,14},{14,8},{16,18},{18,... | collective-permute-start | bytes 786440 | tf_op jit(solution)/shard_map/ppermute | solution.py:37
  28.6 12.2 %collective-permute-start.4 = (bf16[256,512]{1,0:T(8,128)(2,1)S(1)}, bf16[256,512]{1,0:T(8,128)(2,1)S(1)}, u32[]{:S(2)}, u32[]{:S(2)}) collective-permute-start(bf16[256,512]{1,0:T(8,128)(2,1)S(1)} %get-tuple-element.22), channel_id=1, source_target_pairs={{0,6},{2,0},{4,2},{6,4},{8,14},{10,8},{12,10},{14,12},{16,22},{18,... | collective-permute-start | bytes 786440 | tf_op jit(solution)/shard_map/ppermute | solution.py:37
  30.1 21.7 %collective-permute-start.11 = (bf16[256,512]{1,0:T(8,128)(2,1)S(1)}, bf16[256,512]{1,0:T(8,128)(2,1)S(1)}, u32[]{:S(2)}, u32[]{:S(2)}) collective-permute-start(bf16[256,512]{1,0:T(8,128)(2,1)S(1)} %collective-permute-done.10), channel_id=1, source_target_pairs={{0,160},{2,162},{4,164},{6,166},{8,168},{10,170},{12,172},{14,174}... | collective-permute-start | bytes 786440 | tf_op jit(solution)/shard_map/ppermute | solution.py:37
  34.7 17.1 %collective-permute-start.7 = (bf16[256,512]{1,0:T(8,128)(2,1)S(1)}, bf16[256,512]{1,0:T(8,128)(2,1)S(1)}, u32[]{:S(2)}, u32[]{:S(2)}) collective-permute-start(bf16[256,512]{1,0:T(8,128)(2,1)S(1)} %get-tuple-element.24), channel_id=1, source_target_pairs={{0,4},{2,6},{4,0},{6,2},{8,12},{10,14},{12,8},{14,10},{16,20},{18,... | collective-permute-start | bytes 786440 | tf_op jit(solution)/shard_map/ppermute | solution.py:37
  36.0 15.9 %collective-permute-start.9 = (bf16[256,512]{1,0:T(8,128)(2,1)S(1)}, bf16[256,512]{1,0:T(8,128)(2,1)S(1)}, u32[]{:S(2)}, u32[]{:S(2)}) collective-permute-start(bf16[256,512]{1,0:T(8,128)(2,1)S(1)} %collective-permute-done.8.refs_0_), channel_id=1, source_target_pairs={{0,64},{2,66},{4,68},{6,70},{8,72},{10,74},{12,76},{14,78},{16,80}... | collective-permute-start | bytes 786440 | tf_op jit(solution)/shard_map/ppermute | solution.py:37
  40.8 11.0 %collective-permute-start.5 = (bf16[256,512]{1,0:T(8,128)(2,1)S(1)}, bf16[256,512]{1,0:T(8,128)(2,1)S(1)}, u32[]{:S(2)}, u32[]{:S(2)}) collective-permute-start(bf16[256,512]{1,0:T(8,128)(2,1)S(1)} %collective-permute-done.4), channel_id=1, source_target_pairs={{0,6},{2,0},{4,2},{6,4},{8,14},{10,8},{12,10},{14,12},{16,22},{18,... | collective-permute-start | bytes 786440 | tf_op jit(solution)/shard_map/ppermute | solution.py:37
  51.9 19.0 %copy-start = (f32[2048]{0:T(1024)S(1)}, f32[2048]{0:T(1024)}, u32[]{:S(2)}) copy-start(f32[2048]{0:T(1024)} %param.5) | copy-start | bytes 24580
  55.0 15.8 %collective-permute-start.15 = (f32[8,256]{1,0:T(8,128)S(1)}, f32[8,256]{1,0:T(8,128)S(1)}, u32[]{:S(2)}, u32[]{:S(2)}) collective-permute-start(f32[8,256]{1,0:T(8,128)S(1)} %get-tuple-element.34.mine_ref), channel_id=1, source_target_pairs={{0,1},{1,0},{2,3},{3,2},{4,5},{5,4},{6,7},{7,6},{8,9},{9,8},{10,11... | collective-permute-start | bytes 24584 | tf_op jit(solution)/shard_map/ppermute | solution.py:309
